TPU v7x, 32 devices: a whole 2x2x4 slice. The times are simulated.
32 devices in a mesh: parts: 2 (over y), mesh: 4 (over z), tile: 2 (over x), feat: 2 (over core).
Axes of the slice: x: 2, y: 2, z: 4, core: 2. Of those that a mesh axis runs over, the one named last changes fastest.
Arguments:
- fields: bfloat16 [2048, 128], P(('parts', 'mesh', 'tile')), parts along dimension 0, may hold values from -6 to 6
- owner_group: int32 [1024, 1], P(('mesh', 'tile')), may hold values from 0 to 7; in each aligned block of 128 rows (0 to 127, 128 to 255, ...) at most 32 rows name the same one
- owner_node: int32 [1024], P(('mesh', 'tile')), may hold values from 0 to 31
- stencil_codes: int32 [256, 8], P(('mesh', 'tile')), may hold values from 0 to 24
- coarse_ids: int32 [256], P(('mesh', 'tile')), may hold values from 0 to 15
- encode_weight: bfloat16 [128, 512], P(None, 'feat'), may hold values from -0.5 to 0.5
- process_weight: bfloat16 [512, 512], P(None, 'feat'), may hold values from -0.09375 to 0.09375
- coarse_weight: bfloat16 [512, 512], P(None, 'feat'), may hold values from -0.0625 to 0.0625
- decode_weight: bfloat16 [512, 128], P('feat'), may hold values from -0.25 to 0.25
- cotangent: float32 [2048, 128], P(('parts', 'mesh', 'tile')), parts along dimension 0, may hold values from -6 to 6
Outputs:
- prediction: float32 [2048, 128], P(('parts', 'mesh', 'tile')), parts along dimension 0
- encode_grad: float32 [256, 512], P('parts', 'feat'), parts along dimension 0
- process_grad: float32 [1024, 512], P('parts', 'feat'), parts along dimension 0
- coarse_grad: float32 [1024, 512], P('parts', 'feat'), parts along dimension 0
- decode_grad: float32 [1024, 128], P(('parts', 'feat')), parts along dimension 0
There are 2 independent parts, one for each index of `parts`. A program takes and returns all parts, laid end to end along the dimension named above; an argument that names none is the same for every part. Nothing has to cross between parts.
Inputs may be any that keep to these rules, and one draw needn't show every extreme that they name: `owner_group`: in the rows of one device group no value is named more than 32 times.
All inputs are finite; a program needn't handle non-finite values.
Results may differ from a plain program's by a relative error of at most 0.0073.
Values may be sent and summed in bfloat16 or wider, within the bound.
A program may use at most 64 MiB of HBM per device.

v0:
```python
import jax
import jax.numpy as jnp
from jax import lax
from jax.sharding import PartitionSpec as P

MA = 4
MB = 8
CPD = 2


def padded(array, sides, width):
    for axis, dim in sides:
        peers, length = (lax.axis_size(axis), array.shape[dim])
        up = [(i, (i + 1) % peers) for i in range(peers)]
        down = [(j, i) for i, j in up]
        last = lax.slice_in_dim(array, length - width, length, axis=dim)
        initial = lax.slice_in_dim(array, 0, width, axis=dim)
        before = lax.ppermute(last, axis, up)
        after = lax.ppermute(initial, axis, down)
        array = jnp.concatenate([before, array, after], axis=dim)
    return array


def silu_grad(pre):
    sig = jax.nn.sigmoid(pre)
    return sig * (1.0 + pre * (1.0 - sig))


def send_rows(outgoing, slot_node):
    feat_width = outgoing.shape[-1]
    got, got_node = (
        lax.all_to_all(outgoing, ("mesh", "tile"), split_axis=0, concat_axis=0, tiled=True),
        lax.all_to_all(slot_node, ("mesh", "tile"), split_axis=0, concat_axis=0, tiled=True),
    )
    return (got.reshape(-1, feat_width), got_node.reshape(-1))


def route_block(block, mesh_count, tile_count, purpose):
    feat_width = block.shape[-1]
    slot_count = block.shape[0] // (mesh_count * tile_count)
    flat_shape = (mesh_count * tile_count, slot_count, feat_width)
    if purpose == "reply":
        moved = lax.all_to_all(
            block.reshape(flat_shape), ("mesh", "tile"), split_axis=0, concat_axis=0, tiled=True
        )
    elif purpose == "gradient":
        moved = lax.all_to_all(
            block.reshape(flat_shape), ("mesh", "tile"), split_axis=0, concat_axis=0, tiled=True
        )
    else:
        moved = lax.all_to_all(
            block.reshape(flat_shape), ("mesh", "tile"), split_axis=0, concat_axis=0, tiled=True
        )
    return moved.reshape(-1, feat_width)


def body(
    fields,
    owner_group,
    owner_node,
    stencil_codes,
    coarse_ids,
    encode_weight,
    process_weight,
    coarse_weight,
    decode_weight,
    cotangent,
):
    highest = lax.Precision.HIGHEST
    row_count = fields.shape[0]
    mesh_count = lax.axis_size("mesh")
    tile_count = lax.axis_size("tile")
    groups = mesh_count * tile_count
    slot_count = 2 * row_count // groups
    feat_width = encode_weight.shape[1]
    patch_rows = MA
    patch_cols = MB
    nodes_local = patch_rows * patch_cols
    coarse_count = CPD * groups
    target = owner_group[:, 0]
    group_onehot = (target[:, None] == jnp.arange(groups, dtype=jnp.int32)[None, :]).astype(
        jnp.int32
    )
    earlier = jnp.cumsum(group_onehot, axis=0) - group_onehot
    position = target * slot_count + jnp.sum(earlier * group_onehot, axis=1)
    matches = jnp.arange(groups * slot_count, dtype=jnp.int32)[:, None] == position[None, :]
    dispatch = matches.astype(jnp.bfloat16)
    slot_node = (jnp.max(jnp.where(matches, owner_node[None, :] + 1, 0), axis=1) - 1).reshape(
        groups, slot_count
    )
    pre_encode = jnp.dot(fields, encode_weight, preferred_element_type=jnp.float32)
    hidden = jax.nn.silu(pre_encode).astype(jnp.bfloat16)
    outgoing = jnp.dot(dispatch, hidden, preferred_element_type=jnp.float32).astype(jnp.bfloat16)
    incoming, incoming_node = send_rows(outgoing.reshape(groups, slot_count, feat_width), slot_node)
    node_match = (
        incoming_node[:, None] == jnp.arange(nodes_local, dtype=jnp.int32)[None, :]
    ).astype(jnp.bfloat16)
    node_in = jnp.einsum(
        "sn,sh->nh", node_match, incoming, preferred_element_type=jnp.float32
    ).astype(jnp.bfloat16)
    counts = jnp.sum(
        (stencil_codes[:, :, None] == jnp.arange(25, dtype=jnp.int32)[None, None, :]).astype(
            jnp.float32
        ),
        axis=1,
    )
    counts = counts.astype(jnp.bfloat16).reshape(patch_rows, patch_cols, 25)
    padded_nodes, padded_counts = (
        padded(node_in.reshape(patch_rows, patch_cols, feat_width), (("mesh", 0), ("tile", 1)), 2),
        padded(counts, (("mesh", 0), ("tile", 1)), 2),
    )
    gathered = jnp.zeros((patch_rows, patch_cols, feat_width), jnp.float32)
    for code_index in range(25):
        step_x = code_index // 5 - 2
        step_y = code_index % 5 - 2
        weight_here = padded_counts[
            2 : 2 + patch_rows, 2 : 2 + patch_cols, code_index : code_index + 1
        ].astype(jnp.float32)
        gathered = gathered + weight_here * padded_nodes[
            2 + step_x : 2 + step_x + patch_rows, 2 + step_y : 2 + step_y + patch_cols
        ].astype(jnp.float32)
    agg = gathered.reshape(nodes_local, feat_width).astype(jnp.bfloat16)
    agg_full = lax.all_gather(agg, "feat", axis=1, tiled=True)
    pre_mesh = jnp.dot(agg_full, process_weight, preferred_element_type=jnp.float32)
    level_one = node_in.astype(jnp.float32) + jax.nn.silu(pre_mesh)
    coarse_match = (
        coarse_ids[:, None] == jnp.arange(coarse_count, dtype=jnp.int32)[None, :]
    ).astype(jnp.float32)
    coarse_part = jnp.dot(coarse_match.T, level_one, precision=highest)
    coarse_total = lax.psum(coarse_part, ("mesh", "tile"))
    coarse_in = lax.all_gather(coarse_total.astype(jnp.bfloat16), "feat", axis=1, tiled=True)
    pre_coarse = jnp.dot(coarse_in, coarse_weight, preferred_element_type=jnp.float32)
    coarse_out = jax.nn.silu(pre_coarse).astype(jnp.bfloat16)
    level_two = (
        level_one
        + jnp.dot(coarse_match.astype(jnp.bfloat16), coarse_out, preferred_element_type=jnp.float32)
    ).astype(jnp.bfloat16)
    reply_rows = jnp.dot(node_match, level_two, preferred_element_type=jnp.float32).astype(
        jnp.bfloat16
    )
    returned = route_block(reply_rows, mesh_count, tile_count, "reply")
    merged = (
        hidden.astype(jnp.float32)
        + jnp.einsum("sr,sh->rh", dispatch, returned, preferred_element_type=jnp.float32)
    ).astype(jnp.bfloat16)
    pred_part = jnp.dot(merged, decode_weight, preferred_element_type=jnp.float32)
    prediction = lax.psum(pred_part, "feat")
    decode_grad = jnp.dot(merged.astype(jnp.float32).T, cotangent, precision=highest)
    grad_merged = jnp.dot(cotangent, decode_weight.astype(jnp.float32).T, precision=highest)
    grad_out = jnp.dot(
        dispatch, grad_merged.astype(jnp.bfloat16), preferred_element_type=jnp.float32
    ).astype(jnp.bfloat16)
    grad_in = route_block(grad_out, mesh_count, tile_count, "gradient")
    grad_two = jnp.einsum("sn,sh->nh", node_match, grad_in, preferred_element_type=jnp.float32)
    coarse_grad_part = jnp.dot(coarse_match.T, grad_two, precision=highest)
    grad_coarse_out = lax.psum(coarse_grad_part, ("mesh", "tile"))
    grad_pre_coarse = grad_coarse_out * silu_grad(pre_coarse)
    coarse_grad = jnp.dot(coarse_in.astype(jnp.float32).T, grad_pre_coarse, precision=highest)
    grad_coarse_full = jnp.dot(
        grad_pre_coarse, coarse_weight.astype(jnp.float32).T, precision=highest
    )
    grad_coarse_in = lax.psum_scatter(grad_coarse_full, "feat", scatter_dimension=1, tiled=True)
    grad_one = grad_two + jnp.dot(coarse_match, grad_coarse_in, precision=highest)
    grad_pre_mesh = grad_one * silu_grad(pre_mesh)
    process_grad = jnp.dot(agg_full.astype(jnp.float32).T, grad_pre_mesh, precision=highest)
    grad_pre_full = lax.all_gather(grad_pre_mesh, "feat", axis=1, tiled=True)
    weight_full = lax.all_gather(process_weight, "feat", axis=1, tiled=True)
    own_rows = lax.dynamic_slice_in_dim(
        weight_full, lax.axis_index("feat") * feat_width, feat_width, 0
    )
    grad_agg = jnp.dot(grad_pre_full, own_rows.astype(jnp.float32).T, precision=highest).astype(
        jnp.bfloat16
    )
    padded_grad = padded(
        grad_agg.reshape(patch_rows, patch_cols, feat_width), (("mesh", 0), ("tile", 1)), 2
    )
    spread = jnp.zeros((patch_rows, patch_cols, feat_width), jnp.float32)
    for code_index in range(25):
        step_x = code_index // 5 - 2
        step_y = code_index % 5 - 2
        weight_there = padded_counts[
            2 - step_x : 2 - step_x + patch_rows,
            2 - step_y : 2 - step_y + patch_cols,
            code_index : code_index + 1,
        ].astype(jnp.float32)
        spread = spread + weight_there * padded_grad[
            2 - step_x : 2 - step_x + patch_rows, 2 - step_y : 2 - step_y + patch_cols
        ].astype(jnp.float32)
    grad_zero = (grad_one + spread.reshape(nodes_local, feat_width)).astype(jnp.bfloat16)
    back_rows = jnp.dot(node_match, grad_zero, preferred_element_type=jnp.float32).astype(
        jnp.bfloat16
    )
    grad_back = route_block(back_rows, mesh_count, tile_count, "return")
    grad_hidden = grad_merged + jnp.einsum(
        "sr,sh->rh", dispatch, grad_back, preferred_element_type=jnp.float32
    )
    grad_pre_encode = grad_hidden * silu_grad(pre_encode)
    encode_grad = jnp.dot(fields.astype(jnp.float32).T, grad_pre_encode, precision=highest)
    encode_grad, process_grad, decode_grad = lax.psum(
        (encode_grad, process_grad, decode_grad), ("mesh", "tile")
    )
    return (prediction, encode_grad, process_grad, coarse_grad, decode_grad)


def solution(mesh):
    placed = (
        P(("parts", "mesh", "tile"), None),
        P(("mesh", "tile"), None),
        P(("mesh", "tile")),
        P(("mesh", "tile"), None),
        P(("mesh", "tile")),
        P(None, "feat"),
        P(None, "feat"),
        P(None, "feat"),
        P("feat", None),
        P(("parts", "mesh", "tile"), None),
    )
    return jax.shard_map(
        body,
        mesh=mesh,
        in_specs=placed,
        out_specs=(
            P(("parts", "mesh", "tile"), None),
            P("parts", "feat"),
            P("parts", "feat"),
            P("parts", "feat"),
            P(("parts", "feat"), None),
        ),
        check_vma=False,
    )
```

profile of v0, /device:TPU:1, one launch (start us, length us, event | category | flops | bytes accessed | tf_op | source)
XLA Modules:
  0.0 238.7 jit_solution(17337681555565160139)
XLA Ops:
  9.6 6.3 %all-to-all-start = ((s32[8,1,32]{2,1,0:T(1,128)}), s32[8,1,32]{2,1,0:T(1,128)S(1)}, u32[]{:S(2)}, u32[]{:S(2)}) async-start(s32[8,1,32]{2,1,0:T(1,128)} %sub.20), calls=%async_computation | async-start | bytes 8192 | tf_op jit(solution)/shard_map/all_to_all | solution.py:33
  16.2 3.3 %collective-permute-start.5 = (bf16[2,8,25]{2,1,0:T(8,128)(2,1)S(1)}, bf16[2,8,25]{2,1,0:T(8,128)(2,1)S(1)}, u32[]{:S(2)}, u32[]{:S(2)}) collective-permute-start(bf16[2,8,25]{2,1,0:T(8,128)(2,1)S(1)} %bitcast.73), channel_id=1, source_target_pairs={{4,0},{8,4},{12,8},{0,12},{5,1},{9,5},{13,9},{1,13},{6,2},{10,6},{... | collective-permute-start | bytes 2408 | tf_op jit(solution)/shard_map/ppermute | solution.py:19
  21.7 3.3 %all_gather.15 = bf16[512,512]{1,0:T(8,128)(2,1)S(1)} all-gather(bf16[512,256]{1,0:T(8,128)(2,1)S(1)} %copy-done.1), channel_id=1, replica_groups=mesh['parts'=2,'mesh'=4,'tile'=2,'feat'=2] {'feat'}, dimensions={1}, use_global_device_ids=true | all-gather | bytes 786432 | tf_op jit(solution)/shard_map/all_gather | solution.py:167
  27.1 5.7 %all-to-all-start.1 = ((bf16[8,32,256]{2,1,0:T(8,128)(2,1)}), bf16[8,32,256]{2,1,0:T(8,128)(2,1)S(1)}, u32[]{:S(2)}, u32[]{:S(2)}) async-start(bf16[8,32,256]{2,1,0:T(8,128)(2,1)} %bitcast.1), calls=%async_computation.1 | async-start | bytes 262144 | tf_op jit(solution)/shard_map/all_to_all | solution.py:32
  34.4 4.7 %all-to-all-done.1 = bf16[8,32,256]{2,1,0:T(8,128)(2,1)S(1)} async-done(((bf16[8,32,256]{2,1,0:T(8,128)(2,1)}), bf16[8,32,256]{2,1,0:T(8,128)(2,1)S(1)}, u32[]{:S(2)}, u32[]{:S(2)}) %all-to-all-start.1) | async-done | bytes 131104 | tf_op jit(solution)/shard_map/all_to_all | solution.py:32
  39.1 3.4 %all-to-all-start.3 = ((bf16[8,32,256]{2,1,0:T(8,128)(2,1)}), bf16[8,32,256]{2,1,0:T(8,128)(2,1)S(1)}, u32[]{:S(2)}, u32[]{:S(2)}) async-start(bf16[8,32,256]{2,1,0:T(8,128)(2,1)} %bitcast.10), calls=%async_computation.3 | async-start | bytes 262144 | tf_op jit(solution)/shard_map/all_to_all | solution.py:47
  42.7 3.2 %collective-permute-start.1 = (bf16[2,8,256]{2,1,0:T(8,128)(2,1)S(1)}, bf16[2,8,256]{2,1,0:T(8,128)(2,1)S(1)}, u32[]{:S(2)}, u32[]{:S(2)}) collective-permute-start(bf16[2,8,256]{2,1,0:T(8,128)(2,1)S(1)} %get-tuple-element.96), channel_id=1, source_target_pairs={{4,0},{8,4},{12,8},{0,12},{5,1},{9,5},{13,9},{1,13},{6,2},{10,6},{... | collective-permute-start | bytes 24584 | tf_op jit(solution)/shard_map/ppermute | solution.py:19
  45.9 2.6 %all-to-all-done.3 = bf16[8,32,256]{2,1,0:T(8,128)(2,1)S(1)} async-done(((bf16[8,32,256]{2,1,0:T(8,128)(2,1)}), bf16[8,32,256]{2,1,0:T(8,128)(2,1)S(1)}, u32[]{:S(2)}, u32[]{:S(2)}) %all-to-all-start.3) | async-done | bytes 131104 | tf_op jit(solution)/shard_map/all_to_all | solution.py:47
  48.8 1.8 collective-permute-done
  54.4 6.8 %all_gather.12 = bf16[32,512]{1,0:T(8,128)(2,1)S(1)} all-gather(bf16[32,256]{1,0:T(8,128)(2,1)S(1)} %fusion.23), channel_id=1, replica_groups=mesh['parts'=2,'mesh'=4,'tile'=2,'feat'=2] {'feat'}, dimensions={1}, use_global_device_ids=true | all-gather | bytes 49152 | tf_op jit(solution)/shard_map/all_gather | solution.py:123
  61.7 26.2 %all-reduce = (bf16[16,256]{1,0:T(8,128)(2,1)S(1)}, f32[16,256]{1,0:T(8,128)S(1)}) all-reduce(f32[16,256]{1,0:T(8,128)S(1)} %fusion.21, f32[16,256]{1,0:T(8,128)S(1)} %fusion.20), channel_id=1, replica_groups=mesh['parts'=2,'mesh'=4,'tile'=2,'feat'=2] {'mesh','tile'}, use_global_device_ids=true, to_apply=%region_4.5 | all-reduce | flops 8192 | bytes 57344 | tf_op jit(solution)/shard_map/psum | solution.py:130
  87.9 9.0 %all_gather.13 = bf16[16,512]{1,0:T(8,128)(2,1)S(1)} all-gather(bf16[16,256]{1,0:T(8,128)(2,1)S(1)} %get-tuple-element.76), channel_id=1, replica_groups=mesh['parts'=2,'mesh'=4,'tile'=2,'feat'=2] {'feat'}, dimensions={1}, use_global_device_ids=true | all-gather | bytes 24576 | tf_op jit(solution)/shard_map/all_gather | solution.py:131
  98.2 4.8 %reduce-scatter.2.cloned.1.call-done = f32[16,256]{1,0:T(8,128)} async-done(((f32[16,512]{1,0:T(8,128)}), f32[16,256]{1,0:T(8,128)}) %reduce-scatter.2.cloned.1.call-update) | async-done | bytes 16400 | tf_op jit(solution)/shard_map/reduce_scatter | solution.py:162
  103.9 1.9 all_gather.14
  106.1 1.6 collective-permute-start.7
  107.7 1.9 collective-permute-start.8
  110.7 3.6 %all-to-all-start.2 = ((bf16[8,32,256]{2,1,0:T(8,128)(2,1)}), bf16[8,32,256]{2,1,0:T(8,128)(2,1)S(1)}, u32[]{:S(2)}, u32[]{:S(2)}) async-start(bf16[8,32,256]{2,1,0:T(8,128)(2,1)} %bitcast.8), calls=%async_computation.2 | async-start | bytes 262144 | tf_op jit(solution)/shard_map/all_to_all | solution.py:43
  114.3 1.5 collective-permute-start.9
  120.6 3.4 %all-to-all-start.4 = ((bf16[8,32,256]{2,1,0:T(8,128)(2,1)}), bf16[8,32,256]{2,1,0:T(8,128)(2,1)S(1)}, u32[]{:S(2)}, u32[]{:S(2)}) async-start(bf16[8,32,256]{2,1,0:T(8,128)(2,1)} %bitcast.18), calls=%async_computation.5 | async-start | bytes 262144 | tf_op jit(solution)/shard_map/all_to_all | solution.py:51
  125.1 5.0 %all-to-all-done.4 = bf16[8,32,256]{2,1,0:T(8,128)(2,1)S(1)} async-done(((bf16[8,32,256]{2,1,0:T(8,128)(2,1)}), bf16[8,32,256]{2,1,0:T(8,128)(2,1)S(1)}, u32[]{:S(2)}, u32[]{:S(2)}) %all-to-all-start.4) | async-done | bytes 131104 | tf_op jit(solution)/shard_map/all_to_all | solution.py:51
  133.4 73.2 %all-reduce.7.cloned.1.call-done = (f32[128,256]{0,1:T(8,128)}, f32[512,256]{1,0:T(8,128)}, f32[256,128]{1,0:T(8,128)}) async-done(((f32[128,256]{0,1:T(8,128)}, f32[512,256]{1,0:T(8,128)}, f32[256,128]{1,0:T(8,128)}), (f32[128,256]{0,1:T(8,128)}, f32[512,256]{1,0:T(8,128)}, f32[256,128]{1,0:T(8,128)})) %all-reduce.7.cloned.1.call-update) | async-done | bytes 786448 | tf_op jit(solution)/shard_map/psum | solution.py:199
  206.6 1.7 copy.24
  208.3 19.9 %all-reduce.5.cloned.1.call-done = f32[128,128]{1,0:T(8,128)} async-done(((f32[128,128]{1,0:T(8,128)}), f32[128,128]{1,0:T(8,128)}) %all-reduce.5.cloned.1.call-update) | async-done | bytes 65552 | tf_op jit(solution)/shard_map/psum | solution.py:147
  229.6 1.9 copy.30
  (100 shorter events, 28.1 us)
Async XLA Ops:
  7.2 89.7 %copy-start = (bf16[512,256]{1,0:T(8,128)(2,1)S(1)}, bf16[512,256]{1,0:T(8,128)(2,1)}, u32[]{:S(2)}) copy-start(bf16[512,256]{1,0:T(8,128)(2,1)} %param.17) | copy-start | bytes 786436
  8.1 7.8 %copy-start.8 = (s32[32,8]{0,1:T(8,128)S(1)}, s32[32,8]{0,1:T(8,128)}, u32[]{:S(2)}) copy-start(s32[32,8]{0,1:T(8,128)} %param.13) | copy-start | bytes 3076
  8.8 10.8 %copy-start.6 = (bf16[128,256]{1,0:T(8,128)(2,1)S(1)}, bf16[128,256]{1,0:T(8,128)(2,1)}, u32[]{:S(2)}) copy-start(bf16[128,256]{1,0:T(8,128)(2,1)} %param.15) | copy-start | bytes 196612
  9.6 17.5 %all-to-all-start = ((s32[8,1,32]{2,1,0:T(1,128)}), s32[8,1,32]{2,1,0:T(1,128)S(1)}, u32[]{:S(2)}, u32[]{:S(2)}) async-start(s32[8,1,32]{2,1,0:T(1,128)} %sub.20), calls=%async_computation | async-start | bytes 8192 | tf_op jit(solution)/shard_map/all_to_all | solution.py:33
  16.0 3.6 %copy-start.4 = (bf16[128,128]{1,0:T(8,128)(2,1)S(1)}, bf16[128,128]{1,0:T(8,128)(2,1)}, u32[]{:S(2)}) copy-start(bf16[128,128]{1,0:T(8,128)(2,1)} %param.10) | copy-start | bytes 98308
  16.2 9.1 %collective-permute-start.5 = (bf16[2,8,25]{2,1,0:T(8,128)(2,1)S(1)}, bf16[2,8,25]{2,1,0:T(8,128)(2,1)S(1)}, u32[]{:S(2)}, u32[]{:S(2)}) collective-permute-start(bf16[2,8,25]{2,1,0:T(8,128)(2,1)S(1)} %bitcast.73), channel_id=1, source_target_pairs={{4,0},{8,4},{12,8},{0,12},{5,1},{9,5},{13,9},{1,13},{6,2},{10,6},{... | collective-permute-start | bytes 2408 | tf_op jit(solution)/shard_map/ppermute | solution.py:19
  19.5 5.8 %collective-permute-start.4 = (bf16[2,8,25]{2,1,0:T(8,128)(2,1)S(1)}, bf16[2,8,25]{2,1,0:T(8,128)(2,1)S(1)}, u32[]{:S(2)}, u32[]{:S(2)}) collective-permute-start(bf16[2,8,25]{2,1,0:T(8,128)(2,1)S(1)} %bitcast.74), channel_id=1, source_target_pairs={{0,4},{4,8},{8,12},{12,0},{1,5},{5,9},{9,13},{13,1},{2,6},{6,10},{... | collective-permute-start | bytes 2408 | tf_op jit(solution)/shard_map/ppermute | solution.py:18
  25.3 7.5 %collective-permute-start.6 = (bf16[8,2,25]{2,1,0:T(2,128)(2,1)S(1)}, bf16[8,2,25]{2,1,0:T(2,128)(2,1)S(1)}, u32[]{:S(2)}, u32[]{:S(2)}) collective-permute-start(bf16[8,2,25]{2,1,0:T(2,128)(2,1)S(1)} %get-tuple-element.91), channel_id=1, source_target_pairs={{2,0},{0,2},{3,1},{1,3},{6,4},{4,6},{7,5},{5,7},{10,8},{8,10},{11,... | collective-permute-start | bytes 2408 | tf_op jit(solution)/shard_map/ppermute | solution.py:19
  26.6 6.3 %collective-permute-start.10 = (bf16[8,2,25]{2,1,0:T(2,128)(2,1)S(1)}, bf16[8,2,25]{2,1,0:T(2,128)(2,1)S(1)}, u32[]{:S(2)}, u32[]{:S(2)}) collective-permute-start(bf16[8,2,25]{2,1,0:T(2,128)(2,1)S(1)} %get-tuple-element.92), channel_id=1, source_target_pairs={{0,2},{2,0},{1,3},{3,1},{4,6},{6,4},{5,7},{7,5},{8,10},{10,8},{9,1... | collective-permute-start | bytes 2408 | tf_op jit(solution)/shard_map/ppermute | solution.py:18
  27.1 11.9 %all-to-all-start.1 = ((bf16[8,32,256]{2,1,0:T(8,128)(2,1)}), bf16[8,32,256]{2,1,0:T(8,128)(2,1)S(1)}, u32[]{:S(2)}, u32[]{:S(2)}) async-start(bf16[8,32,256]{2,1,0:T(8,128)(2,1)} %bitcast.1), calls=%async_computation.1 | async-start | bytes 262144 | tf_op jit(solution)/shard_map/all_to_all | solution.py:32
  39.1 9.5 %all-to-all-start.3 = ((bf16[8,32,256]{2,1,0:T(8,128)(2,1)}), bf16[8,32,256]{2,1,0:T(8,128)(2,1)S(1)}, u32[]{:S(2)}, u32[]{:S(2)}) async-start(bf16[8,32,256]{2,1,0:T(8,128)(2,1)} %bitcast.10), calls=%async_computation.3 | async-start | bytes 262144 | tf_op jit(solution)/shard_map/all_to_all | solution.py:47
  42.4 60.5 %reduce-scatter.2.cloned.1.call-start = ((), (), s32[]{:S(2)}) async-start(), calls=%async_computation.7 | async-start | bytes 49152 | tf_op jit(solution)/shard_map/reduce_scatter | solution.py:162
  42.7 6.1 %collective-permute-start.1 = (bf16[2,8,256]{2,1,0:T(8,128)(2,1)S(1)}, bf16[2,8,256]{2,1,0:T(8,128)(2,1)S(1)}, u32[]{:S(2)}, u32[]{:S(2)}) collective-permute-start(bf16[2,8,256]{2,1,0:T(8,128)(2,1)S(1)} %get-tuple-element.96), channel_id=1, source_target_pairs={{4,0},{8,4},{12,8},{0,12},{5,1},{9,5},{13,9},{1,13},{6,2},{10,6},{... | collective-permute-start | bytes 24584 | tf_op jit(solution)/shard_map/ppermute | solution.py:19
  45.9 4.7 %collective-permute-start = (bf16[2,8,256]{2,1,0:T(8,128)(2,1)S(1)}, bf16[2,8,256]{2,1,0:T(8,128)(2,1)S(1)}, u32[]{:S(2)}, u32[]{:S(2)}) collective-permute-start(bf16[2,8,256]{2,1,0:T(8,128)(2,1)S(1)} %get-tuple-element.95), channel_id=1, source_target_pairs={{0,4},{4,8},{8,12},{12,0},{1,5},{5,9},{9,13},{13,1},{2,6},{6,10},{... | collective-permute-start | bytes 24584 | tf_op jit(solution)/shard_map/ppermute | solution.py:18
  50.7 2.9 %collective-permute-start.2 = (bf16[8,2,256]{2,1,0:T(2,128)(2,1)S(1)}, bf16[8,2,256]{2,1,0:T(2,128)(2,1)S(1)}, u32[]{:S(2)}, u32[]{:S(2)}) collective-permute-start(bf16[8,2,256]{2,1,0:T(2,128)(2,1)S(1)} %get-tuple-element.87), channel_id=1, source_target_pairs={{0,2},{2,0},{1,3},{3,1},{4,6},{6,4},{5,7},{7,5},{8,10},{10,8},{9,1... | collective-permute-start | bytes 24584 | tf_op jit(solution)/shard_map/ppermute | solution.py:18
  51.7 2.5 %collective-permute-start.3 = (bf16[8,2,256]{2,1,0:T(2,128)(2,1)S(1)}, bf16[8,2,256]{2,1,0:T(2,128)(2,1)S(1)}, u32[]{:S(2)}, u32[]{:S(2)}) collective-permute-start(bf16[8,2,256]{2,1,0:T(2,128)(2,1)S(1)} %get-tuple-element.88), channel_id=1, source_target_pairs={{2,0},{0,2},{3,1},{1,3},{6,4},{4,6},{7,5},{5,7},{10,8},{8,10},{11,... | collective-permute-start | bytes 24584 | tf_op jit(solution)/shard_map/ppermute | solution.py:19
  106.1 8.1 %collective-permute-start.7 = (bf16[2,8,256]{2,1,0:T(8,128)(2,1)S(1)}, bf16[2,8,256]{2,1,0:T(8,128)(2,1)S(1)}, u32[]{:S(2)}, u32[]{:S(2)}) collective-permute-start(bf16[2,8,256]{2,1,0:T(8,128)(2,1)S(1)} %get-tuple-element.94), channel_id=1, source_target_pairs={{0,4},{4,8},{8,12},{12,0},{1,5},{5,9},{9,13},{13,1},{2,6},{6,10},{... | collective-permute-start | bytes 24584 | tf_op jit(solution)/shard_map/ppermute | solution.py:18
  107.7 6.5 %collective-permute-start.8 = (bf16[2,8,256]{2,1,0:T(8,128)(2,1)S(1)}, bf16[2,8,256]{2,1,0:T(8,128)(2,1)S(1)}, u32[]{:S(2)}, u32[]{:S(2)}) collective-permute-start(bf16[2,8,256]{2,1,0:T(8,128)(2,1)S(1)} %get-tuple-element.93), channel_id=1, source_target_pairs={{4,0},{8,4},{12,8},{0,12},{5,1},{9,5},{13,9},{1,13},{6,2},{10,6},{... | collective-permute-start | bytes 24584 | tf_op jit(solution)/shard_map/ppermute | solution.py:19
  110.7 9.9 %all-to-all-start.2 = ((bf16[8,32,256]{2,1,0:T(8,128)(2,1)}), bf16[8,32,256]{2,1,0:T(8,128)(2,1)S(1)}, u32[]{:S(2)}, u32[]{:S(2)}) async-start(bf16[8,32,256]{2,1,0:T(8,128)(2,1)} %bitcast.8), calls=%async_computation.2 | async-start | bytes 262144 | tf_op jit(solution)/shard_map/all_to_all | solution.py:43
  114.3 2.8 %collective-permute-start.9 = (bf16[8,2,256]{2,1,0:T(2,128)(2,1)S(1)}, bf16[8,2,256]{2,1,0:T(2,128)(2,1)S(1)}, u32[]{:S(2)}, u32[]{:S(2)}) collective-permute-start(bf16[8,2,256]{2,1,0:T(2,128)(2,1)S(1)} %get-tuple-element.83), channel_id=1, source_target_pairs={{2,0},{0,2},{3,1},{1,3},{6,4},{4,6},{7,5},{5,7},{10,8},{8,10},{11,... | collective-permute-start | bytes 24584 | tf_op jit(solution)/shard_map/ppermute | solution.py:19
  115.8 2.5 %collective-permute-start.11 = (bf16[8,2,256]{2,1,0:T(2,128)(2,1)S(1)}, bf16[8,2,256]{2,1,0:T(2,128)(2,1)S(1)}, u32[]{:S(2)}, u32[]{:S(2)}) collective-permute-start(bf16[8,2,256]{2,1,0:T(2,128)(2,1)S(1)} %get-tuple-element.84), channel_id=1, source_target_pairs={{0,2},{2,0},{1,3},{3,1},{4,6},{6,4},{5,7},{7,5},{8,10},{10,8},{9,1... | collective-permute-start | bytes 24584 | tf_op jit(solution)/shard_map/ppermute | solution.py:18
  120.6 9.6 %all-to-all-start.4 = ((bf16[8,32,256]{2,1,0:T(8,128)(2,1)}), bf16[8,32,256]{2,1,0:T(8,128)(2,1)S(1)}, u32[]{:S(2)}, u32[]{:S(2)}) async-start(bf16[8,32,256]{2,1,0:T(8,128)(2,1)} %bitcast.18), calls=%async_computation.5 | async-start | bytes 262144 | tf_op jit(solution)/shard_map/all_to_all | solution.py:51
  124.0 82.7 %all-reduce.7.cloned.1.call-start = ((), (), s32[]{:S(2)}) async-start(), calls=%async_computation.8 | async-start | bytes 1572864 | tf_op jit(solution)/shard_map/psum | solution.py:199
  131.4 96.8 %all-reduce.5.cloned.1.call-start = ((), (), s32[]{:S(2)}) async-start(), calls=%async_computation.6 | async-start | bytes 131072 | tf_op jit(solution)/shard_map/psum | solution.py:147
  (7 other events, 7.6 us)
Sparse Core Ops, SparseCore 0:
  98.1 4.8 reduce-scatter.1
  131.5 75.0 all-reduce.6
  209.5 18.6 all-reduce.4
where the time goes:
time: 240 us; the launch traced here: 239 us
  waiting for transfers between devices  116 us (48%)
  blocking collectives  47.2 us (20%)
  starting transfers between devices  37.2 us (16%)
  between operations  14 us (6%)
  matrix products  13.2 us (6%)
  local copies, waits for them, and re-layouts  8.52 us (4%)
  other arithmetic  2.47 us (1%)
    psum x1, waiting for transfers between devices, body(): lax.psum((encode_grad, process_grad, decode_grad), ('mesh', 'tile'))  73.2 us
    psum x1, blocking collectives, body(): coarse_total = lax.psum(coarse_part, ('mesh', 'tile'))  26.2 us
    psum x1, waiting for transfers between devices, body(): prediction = lax.psum(pred_part, 'feat')  19.9 us
    ppermute x6, starting transfers between devices, padded(): after = lax.ppermute(initial, axis, down)  11.6 us
    all_to_all x3, starting transfers between devices, route_block(): lax.all_to_all(block.reshape(flat_shape), ('mesh', 'tile'), split_axis=0,...  10.3 us
    all_gather x1, blocking collectives, body(): lax.all_gather(coarse_total.astype(jnp.bfloat16), 'feat', axis=1, tiled=T...  9.03 us
    all_to_all x3, waiting for transfers between devices, route_block(): lax.all_to_all(block.reshape(flat_shape), ('mesh', 'tile'), split_axis=0,...  8.8 us
    unnamed x26, local copies, waits for them, and re-layouts  6.89 us
  transfers between devices with their start and end apart: 20, of which 11 were waited for; matrix products, arithmetic and copies ran while one was open for 6% of the time, Pallas kernels for 0%

commit v1 on v0

--- a/solution.py
+++ b/solution.py
@@ -1,6 +1,10 @@
+import functools
+
 import jax
 import jax.numpy as jnp
 from jax import lax
+from jax.experimental import pallas as pl
+from jax.experimental.pallas import tpu as pltpu
 from jax.sharding import PartitionSpec as P
 
 MA = 4
@@ -202,6 +206,258 @@
     return (prediction, encode_grad, process_grad, coarse_grad, decode_grad)
 
 
+MESH = pl.DeviceIdType.MESH
+ROW_DIMS = (((0,), (0,)), ((), ()))
+COL_DIMS = (((1,), (1,)), ((), ()))
+EXTRA = 16
+
+
+def gather_kernel(
+    mesh_count, tile_count,
+    packed, enc, proc, coarse, dec,
+    gath, enc_o, proc_o, coarse_o, dec_o,
+    send_sem, recv_sem, pass_send, pass_recv, weight_send, weight_recv, own_sem,
+):
+    groups = mesh_count * tile_count
+    me = lax.axis_index("mesh") * tile_count + lax.axis_index("tile")
+    feat = lax.axis_index("feat")
+    sibling = {"feat": 1 - feat}
+
+    def place(group):
+        return {"mesh": group // tile_count, "tile": group % tile_count}
+
+    barrier = pltpu.get_barrier_semaphore()
+    pl.semaphore_signal(barrier, inc=1, device_id=sibling, device_id_type=MESH)
+    for d in range(1, groups):
+        pl.semaphore_signal(
+            barrier, inc=1, device_id=place((me + d) % groups), device_id_type=MESH
+        )
+    pl.semaphore_wait(barrier, groups)
+    sends = []
+    for d in range(1, groups):
+        copy = pltpu.make_async_remote_copy(
+            src_ref=packed.at[feat], dst_ref=gath.at[me, feat],
+            send_sem=send_sem.at[d], recv_sem=recv_sem.at[d],
+            device_id=place((me + d) % groups), device_id_type=MESH,
+        )
+        copy.start()
+        sends.append(copy)
+    own = pltpu.make_async_copy(packed, gath.at[me], own_sem)
+    own.start()
+    pairs = ((enc, enc_o), (dec, dec_o), (proc, proc_o), (coarse, coarse_o))
+    weights = []
+    for i, (src, dst) in enumerate(pairs):
+        copy = pltpu.make_async_remote_copy(
+            src_ref=src, dst_ref=dst,
+            send_sem=weight_send.at[i], recv_sem=weight_recv.at[i],
+            device_id=sibling, device_id_type=MESH,
+        )
+        copy.start()
+        weights.append(copy)
+    passes = []
+    for d in range(1, groups):
+        sends[d - 1].wait_recv()
+        came = (me - d + groups) % groups
+        copy = pltpu.make_async_remote_copy(
+            src_ref=gath.at[came, feat], dst_ref=gath.at[came, feat],
+            send_sem=pass_send.at[d], recv_sem=pass_recv.at[d],
+            device_id=sibling, device_id_type=MESH,
+        )
+        copy.start()
+        passes.append(copy)
+    own.wait()
+    for copy in sends:
+        copy.wait_send()
+    for copy in weights + passes:
+        copy.wait()
+
+
+def step_kernel(
+    groups, tile_count, nodes, coarse_count,
+    gath, enc_n, proc_n, coarse_n, dec_n, enc_o, proc_o, coarse_o, dec_o,
+    prediction, encode_grad, process_grad, coarse_grad, decode_grad,
+    enc, proc, coarse, dec, pre_s, hid_s, one_s, two_s, gpm_s, gpc_s,
+):
+    f32, b16 = jnp.float32, jnp.bfloat16
+    me = lax.axis_index("mesh") * tile_count + lax.axis_index("tile")
+    feat = lax.axis_index("feat")
+    half = enc_n.shape[1]
+    mine = pl.ds(pl.multiple_of(feat * half, half), half)
+    other = pl.ds(pl.multiple_of((1 - feat) * half, half), half)
+    for full, near, far in ((enc, enc_n, enc_o), (proc, proc_n, proc_o), (coarse, coarse_n, coarse_o)):
+        full[:, mine] = near[...]
+        full[:, other] = far[...]
+    dec[mine, :] = dec_n[...]
+    dec[other, :] = dec_o[...]
+
+    c_in = enc_n.shape[0]
+    part_rows = gath.shape[2] - EXTRA
+    row_count = 2 * part_rows
+
+    def dot(a, b):
+        return jnp.dot(a, b, preferred_element_type=f32)
+
+    def row_dot(a, b):
+        return lax.dot_general(a, b, ROW_DIMS, preferred_element_type=f32)
+
+    def col_dot(a, b):
+        return lax.dot_general(a, b, COL_DIMS, preferred_element_type=f32)
+
+    def onehot(ids, count):
+        numbers = lax.broadcasted_iota(jnp.int32, (count, ids.shape[1]), 0)
+        return jnp.where(numbers == ids, 1.0, 0.0)
+
+    def targets(group):
+        return gath[group, 0, part_rows:, :][:1, :row_count].astype(f32).astype(jnp.int32)
+
+    pieces = [gath[g, h, :part_rows, :] for g in range(groups) for h in range(2)]
+    cells = jnp.concatenate([p[:, :c_in] for p in pieces], axis=0)
+    cot = jnp.concatenate([p[:, c_in:] for p in pieces], axis=0)
+    attach = jnp.concatenate(
+        [onehot(targets(g), nodes).astype(b16) for g in range(groups)], axis=1
+    )
+    extra = gath[0, 1, part_rows:, :].astype(f32)
+    for g in range(1, groups):
+        extra = extra + gath[g, 1, part_rows:, :].astype(f32)
+    ids = extra[:, :nodes].astype(jnp.int32)
+    edges = onehot(ids[0:1], nodes)
+    for k in range(1, 8):
+        edges = edges + onehot(ids[k : k + 1], nodes)
+    edges = edges.astype(b16)
+    to_coarse = onehot(ids[8:9], coarse_count).astype(b16)
+
+    pre = dot(cells, enc[...])
+    pre_s[...] = pre
+    hidden = (pre * jax.nn.sigmoid(pre)).astype(b16)
+    hid_s[...] = hidden
+    node_in = dot(attach, hidden).astype(b16)
+    node_cot = dot(attach, cot).astype(b16)
+    agg = row_dot(edges, node_in).astype(b16)
+    pre_mesh = dot(agg, proc[...])
+    sig_mesh = jax.nn.sigmoid(pre_mesh)
+    level_one = node_in.astype(f32) + pre_mesh * sig_mesh
+    upper = level_one.astype(b16)
+    lower = (level_one - upper.astype(f32)).astype(b16)
+    coarse_in = (dot(to_coarse, upper) + dot(to_coarse, lower)).astype(b16)
+    pre_coarse = dot(coarse_in, coarse[...])
+    sig_coarse = jax.nn.sigmoid(pre_coarse)
+    coarse_out = (pre_coarse * sig_coarse).astype(b16)
+    level_two = (level_one + row_dot(to_coarse, coarse_out)).astype(b16)
+    two_s[...] = level_two
+
+    own_cells = jnp.concatenate([gath[me, h, :part_rows, :c_in] for h in range(2)], axis=0)
+    own_attach = onehot(targets(me), nodes).astype(b16)
+    own_pre = dot(own_cells, enc[...])
+    own_hidden = (own_pre * jax.nn.sigmoid(own_pre)).astype(b16)
+    merged = (own_hidden.astype(f32) + row_dot(own_attach, level_two)).astype(b16)
+    prediction[...] = dot(merged, dec[...])
+    decode_grad[...] = row_dot(hid_s[:, mine], cot) + row_dot(two_s[:, mine], node_cot)
+
+    grad_two = col_dot(node_cot, dec[...])
+    coarse_cot = dot(to_coarse, node_cot).astype(b16)
+    grad_coarse_out = col_dot(coarse_cot, dec[...])
+    grad_pre_coarse = grad_coarse_out * (
+        sig_coarse * (1.0 + pre_coarse * (1.0 - sig_coarse))
+    )
+    gpc = grad_pre_coarse.astype(b16)
+    gpc_s[...] = gpc
+    coarse_grad[...] = row_dot(coarse_in, gpc_s[:, mine])
+    grad_coarse_in = col_dot(gpc, coarse[...]).astype(b16)
+    grad_one = grad_two + row_dot(to_coarse, grad_coarse_in)
+    one_s[...] = grad_one
+    gpm = (grad_one * (sig_mesh * (1.0 + pre_mesh * (1.0 - sig_mesh)))).astype(b16)
+    gpm_s[...] = gpm
+    process_grad[...] = row_dot(agg, gpm_s[:, mine])
+    grad_agg = col_dot(gpm, proc[mine, :]).astype(b16)
+    grad_zero = (one_s[:, mine] + dot(edges, grad_agg)).astype(b16)
+    grad_hidden = col_dot(cot, dec[mine, :]) + row_dot(attach, grad_zero)
+    pre_own = pre_s[:, mine]
+    sig_own = jax.nn.sigmoid(pre_own)
+    grad_pre = (grad_hidden * (sig_own * (1.0 + pre_own * (1.0 - sig_own)))).astype(b16)
+    encode_grad[...] = row_dot(cells, grad_pre)
+
+
+def replicated_body(
+    fields, owner_group, owner_node, stencil_codes, coarse_ids,
+    encode_weight, process_weight, coarse_weight, decode_weight, cotangent,
+):
+    f32, b16 = jnp.float32, jnp.bfloat16
+    mesh_count, tile_count = lax.axis_size("mesh"), lax.axis_size("tile")
+    groups = mesh_count * tile_count
+    nodes_local = MA * MB
+    nodes = nodes_local * groups
+    m, t = lax.axis_index("mesh"), lax.axis_index("tile")
+    me = m * tile_count + t
+    row_count, c_in = fields.shape
+    c_out = cotangent.shape[1]
+    width = c_in + c_out
+    half = encode_weight.shape[1]
+    full = process_weight.shape[0]
+
+    target = owner_group[:, 0] * nodes_local + owner_node
+    local = jnp.arange(nodes_local, dtype=jnp.int32)[None, :]
+    codes = stencil_codes.T
+    row = (m * MA + local // MB + codes // 5 - 2) % (mesh_count * MA)
+    col = (t * MB + local % MB + codes % 5 - 2) % (tile_count * MB)
+    near = (row // MA * tile_count + col // MB) * nodes_local + row % MA * MB + col % MB
+    ids = jnp.concatenate(
+        [near, coarse_ids[None, :], jnp.zeros((EXTRA - 9, nodes_local), jnp.int32)], axis=0
+    )
+    lanes = jnp.arange(width, dtype=jnp.int32)[None, :] // nodes_local
+    spread = jnp.where(lanes == me, jnp.tile(ids, (1, width // nodes_local)), 0).astype(b16)
+    named = jnp.pad(target[None, :], ((0, EXTRA - 1), (0, width - row_count))).astype(b16)
+    both = jnp.concatenate([fields, cotangent.astype(b16)], axis=1)
+    part_rows = row_count // 2
+    packed = jnp.stack(
+        [
+            jnp.concatenate([both[:part_rows], named], axis=0),
+            jnp.concatenate([both[part_rows:], spread], axis=0),
+        ]
+    )
+    any_spec = pl.BlockSpec(memory_space=pl.ANY)
+    vmem = pl.BlockSpec(memory_space=pltpu.VMEM)
+    like = lambda a: jax.ShapeDtypeStruct(a.shape, a.dtype)
+    own = (encode_weight, process_weight, coarse_weight, decode_weight)
+    gath, *others = pl.pallas_call(
+        functools.partial(gather_kernel, mesh_count, tile_count),
+        out_shape=[jax.ShapeDtypeStruct((groups,) + packed.shape, b16)] + [like(w) for w in own],
+        in_specs=[vmem] + [any_spec] * 4,
+        out_specs=[any_spec] * 5,
+        scratch_shapes=[pltpu.SemaphoreType.DMA((groups,))] * 4
+        + [pltpu.SemaphoreType.DMA((4,))] * 2
+        + [pltpu.SemaphoreType.DMA],
+        compiler_params=pltpu.CompilerParams(collective_id=0, has_side_effects=True),
+        name="gather",
+    )(packed, *own)
+    coarse_count = CPD * groups
+    total_rows = row_count * groups
+    shape = lambda *dims: jax.ShapeDtypeStruct(dims, f32)
+    return tuple(
+        pl.pallas_call(
+            functools.partial(step_kernel, groups, tile_count, nodes, coarse_count),
+            out_shape=[
+                shape(row_count, c_out), shape(c_in, half), shape(full, half),
+                shape(full, half), shape(half, c_out),
+            ],
+            in_specs=[vmem] * 9,
+            out_specs=[vmem] * 5,
+            scratch_shapes=[
+                pltpu.VMEM((c_in, full), b16),
+                pltpu.VMEM((full, full), b16),
+                pltpu.VMEM((full, full), b16),
+                pltpu.VMEM((full, c_out), b16),
+                pltpu.VMEM((total_rows, full), f32),
+                pltpu.VMEM((total_rows, full), b16),
+                pltpu.VMEM((nodes, full), f32),
+                pltpu.VMEM((nodes, full), b16),
+                pltpu.VMEM((nodes, full), b16),
+                pltpu.VMEM((coarse_count, full), b16),
+            ],
+            name="step",
+        )(gath, *own, *others)
+    )
+
+
 def solution(mesh):
     placed = (
         P(("parts", "mesh", "tile"), None),
@@ -215,8 +471,10 @@
         P("feat", None),
         P(("parts", "mesh", "tile"), None),
     )
+    groups = mesh.shape["mesh"] * mesh.shape["tile"]
+    fits = MA * MB * groups <= 256
     return jax.shard_map(
-        body,
+        replicated_body if fits else body,
         mesh=mesh,
         in_specs=placed,
         out_specs=(

time: 240 us -> 25.6 us (0.11)
  waiting for transfers between devices: 116 us -> 0 us
  blocking collectives: 47.2 us -> 0 us
  starting transfers between devices: 37.2 us -> 0 us
  Pallas kernels: 0 us -> 21.4 us
  between operations: 14 us -> 0.73 us
  matrix products: 13.2 us -> 0 us
  local copies, waits for them, and re-layouts: 8.52 us -> 1.44 us
    psum x2 -> x0, waiting for transfers between devices: 93.1 us -> none  [the longest x1 73.2 us: body(): lax.psum((encode_grad, process_grad, decode_grad), ('mesh', 'tile'))]
    psum x1 -> x0, blocking collectives: 26.2 us -> none  [body(): coarse_total = lax.psum(coarse_part, ('mesh', 'tile'))]
    all_to_all x5 -> x0, starting transfers between devices: 22.4 us -> none  [the longest x3 10.3 us: route_block(): lax.all_to_all(block.reshape(flat_shape), ('mesh', 'tile'), split_axis=0,...]
    pallas_call x0 -> x2, Pallas kernels: none -> 21.4 us  [the longest x1 14.5 us: replicated_body(): pl.pallas_call(functools.partial(gather_kernel, mesh_count, tile_count),...]
    all_gather x4 -> x0, blocking collectives: 21 us -> none  [the longest x1 9.03 us: body(): lax.all_gather(coarse_total.astype(jnp.bfloat16), 'feat', axis=1, tiled=T...]
    ppermute x12 -> x0, starting transfers between devices: 14.7 us -> none  [the longest x6 11.6 us: padded(): after = lax.ppermute(initial, axis, down)]
    all_to_all x5 -> x0, waiting for transfers between devices: 13.5 us -> none  [the longest x3 8.8 us: route_block(): lax.all_to_all(block.reshape(flat_shape), ('mesh', 'tile'), split_axis=0,...]
    dot_general x22 -> x0, matrix products: 13.2 us -> none  [the longest x1 1.21 us: body(): jnp.dot(agg_full.astype(jnp.float32).T, grad_pre_mesh, precision=highest)]
  transfers between devices with their start and end apart: 20 -> 0, of which waited for: 11 -> 0; matrix products, arithmetic and copies ran while one was open for 6% -> 0% of each run, Pallas kernels for 0% -> 0%
where the time goes in v1:
time: 25.6 us; the launch traced here: 25.3 us
  Pallas kernels  21.4 us (84%)
  other arithmetic  1.65 us (6%)
  local copies, waits for them, and re-layouts  1.44 us (6%)
  between operations  0.73 us (3%)
    pallas_call x1, Pallas kernels, replicated_body(): pl.pallas_call(functools.partial(gather_kernel, mesh_count, tile_count),...  14.5 us
    pallas_call x1, Pallas kernels, replicated_body(): pl.pallas_call(functools.partial(step_kernel, groups, tile_count, nodes,...  6.93 us
    unnamed x10, local copies, waits for them, and re-layouts  1.27 us
    convert_element_type x1, other arithmetic, replicated_body(): both = jnp.concatenate([fields, cotangent.astype(b16)], axis=1)  0.85 us
    another operation x3, other arithmetic, replicated_body(): jnp.stack([jnp.concatenate([both[:part_rows], named], axis=0), jnp.concat...  0.66 us

profile of v1, /device:TPU:1, one launch (start us, length us, event | category | flops | bytes accessed | tf_op | source)
XLA Modules:
  0.0 25.3 jit_solution(2353417267237503082)
XLA Ops:
  0.7 0.0 copy-start.3
  0.7 0.0 copy-start.4
  0.7 0.0 copy-start.1
  0.7 0.6 %copy-done.3 = s32[128]{0:T(128)S(1)} copy-done((s32[128]{0:T(128)S(1)}, s32[128]{0:T(128)}, u32[]{:S(2)}) %copy-start.3) | copy-done | bytes 536
  1.3 0.0 copy-done.4
  1.3 0.1 pad.12.clone
  1.4 0.0 copy-done.1
  1.4 0.0 copy-start.2
  1.5 0.6 %copy-done.2 = s32[32]{0:T(128)S(1)} copy-done((s32[32]{0:T(128)S(1)}, s32[32]{0:T(128)}, u32[]{:S(2)}) %copy-start.2) | copy-done | bytes 152
  2.1 0.1 add_add_fusion
  2.2 0.0 copy-start
  2.2 0.9 %convert_element_type.7 = bf16[128,128]{1,0:T(8,128)(2,1)S(1)} convert(f32[128,128]{1,0:T(8,128)} %param.19) | non-fusion elementwise | flops 16384 | bytes 98304 | tf_op jit(solution)/shard_map/convert_element_type | solution.py:409
  3.0 0.0 copy-done
  3.1 0.1 tile.10
  3.2 0.6 %pad_maximum_fusion.packed = bf16[2,80,256]{2,1,0:T(8,128)(2,1)} fusion(bf16[1,80,256]{2,1,0:T(8,128)(2,1)S(1)} %fusion.4, bf16[1,80,256]{2,1,0:T(8,128)(2,1)S(1)} %fusion.2), kind=kLoop, calls=%fused_computation.1 | loop fusion | flops 40960 | bytes 163840 | tf_op jit(solution)/shard_map/stack | solution.py:411
  3.8 14.5 %gather.1 = (bf16[8,2,80,256]{3,2,1,0:T(8,128)(2,1)}, bf16[128,256]{1,0:T(8,128)(2,1)}, bf16[512,256]{1,0:T(8,128)(2,1)}, bf16[512,256]{1,0:T(8,128)(2,1)}, bf16[256,128]{1,0:T(8,128)(2,1)}) custom-call(bf16[2,80,256]{2,1,0:T(8,128)(2,1)} %pad_maximum_fusion.packed, bf16[128,256]{1,0:T(8,128)(2,1)} %enc_n.1, bf16[512,256]{1,0:T(8,128)(2,1)} %proc_n.1, ...), custom_call_target="tpu_custom_call" | custom-call | tf_op jit(solution)/shard_map/gather/pallas_call | solution.py:421
  18.3 6.9 %step.1 = (f32[128,128]{1,0:T(8,128)}, f32[128,256]{1,0:T(8,128)}, f32[512,256]{1,0:T(8,128)}, f32[512,256]{1,0:T(8,128)}, f32[256,128]{1,0:T(8,128)}) custom-call(bf16[8,2,80,256]{3,2,1,0:T(8,128)(2,1)} %get-tuple-element.10.gath, bf16[128,256]{1,0:T(8,128)(2,1)} %enc_n.1, bf16[512,256]{1,0:T(8,128)(2,1)} %proc_n.1, bf16[512,256]{1,0:T(8,128)(2,1)} %coarse_n.1, ...), custom_call_target="tpu_custom_call" | custom-call | tf_op jit(solution)/shard_map/step/pallas_call | solution.py:436
  (10 shorter events, 0.1 us)
Async XLA Ops:
  0.7 0.7 %copy-start.3 = (s32[128]{0:T(128)S(1)}, s32[128]{0:T(128)}, u32[]{:S(2)}) copy-start(s32[128]{0:T(128)} %param.12) | copy-start | bytes 1540
  0.7 0.7 %copy-start.4 = (s32[128,1]{0,1:T(1,128)S(1)}, s32[128,1]{0,1:T(1,128)}, u32[]{:S(2)}) copy-start(s32[128,1]{0,1:T(1,128)} %param.11) | copy-start | bytes 1540
  0.7 0.7 %copy-start.1 = (s32[32,8]{0,1:T(8,128)S(1)}, s32[32,8]{0,1:T(8,128)}, u32[]{:S(2)}) copy-start(s32[32,8]{0,1:T(8,128)} %param.13) | copy-start | bytes 3076
  1.4 0.7 %copy-start.2 = (s32[32]{0:T(128)S(1)}, s32[32]{0:T(128)}, u32[]{:S(2)}) copy-start(s32[32]{0:T(128)} %param.14) | copy-start | bytes 388
  2.2 0.9 %copy-start = (bf16[128,128]{1,0:T(8,128)(2,1)S(1)}, bf16[128,128]{1,0:T(8,128)(2,1)}, u32[]{:S(2)}) copy-start(bf16[128,128]{1,0:T(8,128)(2,1)} %param.10) | copy-start | bytes 98308

commit v2 on v0

--- a/solution.py
+++ b/solution.py
@@ -1,6 +1,10 @@
+import functools
+
 import jax
 import jax.numpy as jnp
 from jax import lax
+from jax.experimental import pallas as pl
+from jax.experimental.pallas import tpu as pltpu
 from jax.sharding import PartitionSpec as P
 
 MA = 4
@@ -202,6 +206,290 @@
     return (prediction, encode_grad, process_grad, coarse_grad, decode_grad)
 
 
+MESH = pl.DeviceIdType.MESH
+ROW_DIMS = (((0,), (0,)), ((), ()))
+COL_DIMS = (((1,), (1,)), ((), ()))
+EXTRA = 8
+
+
+def quotient(values, divisor):
+    return jnp.floor((values.astype(jnp.float32) + 0.5) * (1.0 / divisor)).astype(jnp.int32)
+
+
+def onehot(ids, count):
+    numbers = lax.broadcasted_iota(jnp.int32, (count, ids.shape[1]), 0)
+    return jnp.where(numbers == ids, 1.0, 0.0)
+
+
+def dot(a, b):
+    return jnp.dot(a, b, preferred_element_type=jnp.float32)
+
+
+def row_dot(a, b):
+    return lax.dot_general(a, b, ROW_DIMS, preferred_element_type=jnp.float32)
+
+
+def col_dot(a, b):
+    return lax.dot_general(a, b, COL_DIMS, preferred_element_type=jnp.float32)
+
+
+def step_kernel(
+    mesh_count, tile_count,
+    fields, owner_group, owner_node, codes, coarse_ids, cotangent,
+    enc_n, proc_n, coarse_n, dec_n,
+    prediction, encode_grad, process_grad, coarse_grad, decode_grad,
+    gath, enc, proc, coarse, dec, cells, cot, attach, pre_s, hid_s, base_s, one_s, two_s, gpm_s, gpc_s,
+    send_sem, recv_sem, pass_send, pass_recv, weight_send, weight_recv, local_sem,
+):
+    f32, b16 = jnp.float32, jnp.bfloat16
+    groups = mesh_count * tile_count
+    m, t, feat = lax.axis_index("mesh"), lax.axis_index("tile"), lax.axis_index("feat")
+    me = m * tile_count + t
+    sibling = {"feat": 1 - feat}
+    nodes_local = MA * MB
+    nodes = nodes_local * groups
+    coarse_count = CPD * groups
+    row_count, c_in = fields.shape
+    width = c_in + cotangent.shape[1]
+    part_rows = row_count // 2
+    half = enc_n.shape[1]
+    mine = pl.ds(pl.multiple_of(feat * half, half), half)
+
+    def place(group):
+        return {"mesh": group // tile_count, "tile": group % tile_count}
+
+    barrier = pltpu.get_barrier_semaphore()
+    pl.semaphore_signal(barrier, inc=1, device_id=sibling, device_id_type=MESH)
+    for d in range(1, groups):
+        pl.semaphore_signal(
+            barrier, inc=1, device_id=place((me + d) % groups), device_id_type=MESH
+        )
+
+    pairs = (
+        (enc_n, enc.at[:, mine]), (dec_n, dec.at[mine, :]),
+        (proc_n, proc.at[:, mine]), (coarse_n, coarse.at[:, mine]),
+    )
+    locals_ = []
+    for i, (src, dst) in enumerate(pairs):
+        copy = pltpu.make_async_copy(src, dst, local_sem.at[i])
+        copy.start()
+        locals_.append(copy)
+
+    both = jnp.concatenate([fields[...], cotangent[...].astype(b16)], axis=1)
+    gath[me, 0, :part_rows, :] = both[:part_rows]
+    gath[me, 1, :part_rows, :] = both[part_rows:]
+    code = codes[...]
+    code_row = sum(jnp.where(code >= 5 * i, 1, 0) for i in range(1, 5))
+    local = lax.broadcasted_iota(jnp.int32, (1, nodes_local), 1)
+    local_row = quotient(local, MB)
+    row = m * MA + local_row + code_row - 2
+    col = t * MB + (local - local_row * MB) + (code - 5 * code_row) - 2
+    rows_all, cols_all = mesh_count * MA, tile_count * MB
+    for _ in range(2):
+        row = jnp.where(row < 0, row + rows_all, jnp.where(row >= rows_all, row - rows_all, row))
+        col = jnp.where(col < 0, col + cols_all, jnp.where(col >= cols_all, col - cols_all, col))
+    row_group, col_group = quotient(row, MA), quotient(col, MB)
+    near = (
+        (row_group * tile_count + col_group) * nodes_local
+        + (row - row_group * MA) * MB + col - col_group * MB
+    )
+    spot = jnp.where(
+        lax.broadcasted_iota(jnp.int32, (nodes_local, width), 1)
+        == lax.broadcasted_iota(jnp.int32, (nodes_local, width), 0) + nodes_local * me,
+        1.0, 0.0,
+    ).astype(b16)
+    order = lax.broadcasted_iota(jnp.int32, (EXTRA, nodes_local), 0)
+    owned = jnp.where(order == 1, coarse_ids[...], 0).astype(f32).astype(b16)
+    owned = dot(owned, spot)
+    target = (owner_group[...] * nodes_local + owner_node[...]).astype(f32)
+    order = lax.broadcasted_iota(jnp.int32, (EXTRA, row_count), 0)
+    named = jnp.where(order == 0, target, owned[:, :row_count])
+    gath[me, 0, part_rows:, :] = jnp.concatenate([named, owned[:, row_count:]], axis=1).astype(b16)
+    gath[me, 1, part_rows:, :] = dot(near.astype(f32).astype(b16), spot).astype(b16)
+
+    pl.semaphore_wait(barrier, groups)
+    sends = []
+    for d in range(1, groups):
+        copy = pltpu.make_async_remote_copy(
+            src_ref=gath.at[me, feat], dst_ref=gath.at[me, feat],
+            send_sem=send_sem.at[d], recv_sem=recv_sem.at[d],
+            device_id=place((me + d) % groups), device_id_type=MESH,
+        )
+        copy.start()
+        sends.append(copy)
+    weights = []
+    for i, (src, dst) in enumerate(pairs):
+        copy = pltpu.make_async_remote_copy(
+            src_ref=src, dst_ref=dst,
+            send_sem=weight_send.at[i], recv_sem=weight_recv.at[i],
+            device_id=sibling, device_id_type=MESH,
+        )
+        copy.start()
+        weights.append(copy)
+
+    def take(g):
+        rows = pl.ds(pl.multiple_of(g * row_count, row_count), row_count)
+        block = jnp.concatenate([gath[g, h, :part_rows, :] for h in range(2)], axis=0)
+        x, c = block[:, :c_in], block[:, c_in:]
+        cells[rows, :] = x
+        cot[rows, :] = c
+        ids = gath[g, 0, part_rows:, :][:1, :row_count].astype(f32).astype(jnp.int32)
+        attach[:, rows] = onehot(ids, nodes).astype(b16)
+        pre = dot(x, enc[...])
+        pre_s[rows, :] = pre
+        hid_s[rows, :] = (pre * jax.nn.sigmoid(pre)).astype(b16)
+        base_s[rows, :] = col_dot(c, dec[mine, :])
+
+    for i in range(2):
+        locals_[i].wait()
+        weights[i].wait_recv()
+    passes = []
+    take(me)
+    for d in range(1, groups):
+        sends[d - 1].wait_recv()
+        came = (me - d + groups) % groups
+        copy = pltpu.make_async_remote_copy(
+            src_ref=gath.at[came, feat], dst_ref=gath.at[came, feat],
+            send_sem=pass_send.at[d], recv_sem=pass_recv.at[d],
+            device_id=sibling, device_id_type=MESH,
+        )
+        copy.start()
+        passes.append(copy)
+        if d > 1:
+            passes[d - 2].wait_recv()
+            take((me - d + 1 + groups) % groups)
+    passes[groups - 2].wait_recv()
+    take((me + 1) % groups)
+
+    node_in = dot(attach[...], hid_s[...]).astype(b16)
+    node_cot = dot(attach[...], cot[...]).astype(b16)
+    owned = gath[0, 0, part_rows:, :].astype(f32)
+    linked = gath[0, 1, part_rows:, :].astype(f32)
+    for g in range(1, groups):
+        owned = owned + gath[g, 0, part_rows:, :].astype(f32)
+        linked = linked + gath[g, 1, part_rows:, :].astype(f32)
+    linked = linked[:, :nodes].astype(jnp.int32)
+    edges = onehot(linked[0:1], nodes)
+    for k in range(1, linked.shape[0]):
+        edges = edges + onehot(linked[k : k + 1], nodes)
+    edges = edges.astype(b16)
+    to_coarse = onehot(owned[1:2, :nodes].astype(jnp.int32), coarse_count).astype(b16)
+
+    agg = row_dot(edges, node_in).astype(b16)
+    locals_[2].wait()
+    weights[2].wait_recv()
+    pre_mesh = dot(agg, proc[...])
+    sig_mesh = jax.nn.sigmoid(pre_mesh)
+    level_one = node_in.astype(f32) + pre_mesh * sig_mesh
+    upper = level_one.astype(b16)
+    lower = (level_one - upper.astype(f32)).astype(b16)
+    coarse_in = (dot(to_coarse, upper) + dot(to_coarse, lower)).astype(b16)
+    locals_[3].wait()
+    weights[3].wait_recv()
+    pre_coarse = dot(coarse_in, coarse[...])
+    sig_coarse = jax.nn.sigmoid(pre_coarse)
+    coarse_out = (pre_coarse * sig_coarse).astype(b16)
+    level_two = (level_one + row_dot(to_coarse, coarse_out)).astype(b16)
+    two_s[...] = level_two
+
+    own_rows = pl.ds(pl.multiple_of(me * row_count, row_count), row_count)
+    merged = (
+        hid_s[own_rows, :].astype(f32) + row_dot(attach[:, own_rows], level_two)
+    ).astype(b16)
+    prediction[...] = dot(merged, dec[...])
+    decode_grad[...] = row_dot(hid_s[:, mine], cot[...]) + row_dot(two_s[:, mine], node_cot)
+
+    grad_two = col_dot(node_cot, dec[...])
+    coarse_cot = dot(to_coarse, node_cot).astype(b16)
+    grad_coarse_out = col_dot(coarse_cot, dec[...])
+    grad_pre_coarse = grad_coarse_out * (
+        sig_coarse * (1.0 + pre_coarse * (1.0 - sig_coarse))
+    )
+    gpc = grad_pre_coarse.astype(b16)
+    gpc_s[...] = gpc
+    coarse_grad[...] = row_dot(coarse_in, gpc_s[:, mine])
+    grad_coarse_in = col_dot(gpc, coarse[...]).astype(b16)
+    grad_one = grad_two + row_dot(to_coarse, grad_coarse_in)
+    one_s[...] = grad_one
+    gpm = (grad_one * (sig_mesh * (1.0 + pre_mesh * (1.0 - sig_mesh)))).astype(b16)
+    gpm_s[...] = gpm
+    process_grad[...] = row_dot(agg, gpm_s[:, mine])
+    grad_agg = col_dot(gpm, proc[mine, :]).astype(b16)
+    grad_zero = (one_s[:, mine] + dot(edges, grad_agg)).astype(b16)
+    grad_hidden = base_s[...] + row_dot(attach[...], grad_zero)
+    pre_own = pre_s[:, mine]
+    sig_own = jax.nn.sigmoid(pre_own)
+    grad_pre = (grad_hidden * (sig_own * (1.0 + pre_own * (1.0 - sig_own)))).astype(b16)
+    encode_grad[...] = row_dot(cells[...], grad_pre)
+
+    for copy in sends + passes + weights:
+        copy.wait_send()
+
+
+def replicated_body(
+    fields, owner_group, owner_node, stencil_codes, coarse_ids,
+    encode_weight, process_weight, coarse_weight, decode_weight, cotangent,
+):
+    f32, b16 = jnp.float32, jnp.bfloat16
+    mesh_count, tile_count = lax.axis_size("mesh"), lax.axis_size("tile")
+    groups = mesh_count * tile_count
+    nodes = MA * MB * groups
+    row_count, c_in = fields.shape
+    c_out = cotangent.shape[1]
+    half = encode_weight.shape[1]
+    full = process_weight.shape[0]
+    coarse_count = CPD * groups
+    total_rows = row_count * groups
+    any_spec = pl.BlockSpec(memory_space=pl.ANY)
+    vmem = pl.BlockSpec(memory_space=pltpu.VMEM)
+    shape = lambda *dims: jax.ShapeDtypeStruct(dims, f32)
+    return tuple(
+        pl.pallas_call(
+            functools.partial(step_kernel, mesh_count, tile_count),
+            out_shape=[
+                shape(row_count, c_out), shape(c_in, half), shape(full, half),
+                shape(full, half), shape(half, c_out),
+            ],
+            in_specs=[vmem] * 6 + [any_spec] * 4,
+            out_specs=[vmem] * 5,
+            scratch_shapes=[
+                pltpu.VMEM((groups, 2, row_count // 2 + EXTRA, c_in + c_out), b16),
+                pltpu.VMEM((c_in, full), b16),
+                pltpu.VMEM((full, full), b16),
+                pltpu.VMEM((full, full), b16),
+                pltpu.VMEM((full, c_out), b16),
+                pltpu.VMEM((total_rows, c_in), b16),
+                pltpu.VMEM((total_rows, c_out), b16),
+                pltpu.VMEM((nodes, total_rows), b16),
+                pltpu.VMEM((total_rows, full), f32),
+                pltpu.VMEM((total_rows, full), b16),
+                pltpu.VMEM((total_rows, half), f32),
+                pltpu.VMEM((nodes, full), f32),
+                pltpu.VMEM((nodes, full), b16),
+                pltpu.VMEM((nodes, full), b16),
+                pltpu.VMEM((coarse_count, full), b16),
+            ]
+            + [pltpu.SemaphoreType.DMA((groups,))] * 4
+            + [pltpu.SemaphoreType.DMA((4,))] * 3,
+            compiler_params=pltpu.CompilerParams(collective_id=0, has_side_effects=True),
+            name="step",
+        )(
+            fields, owner_group.reshape(1, -1), owner_node.reshape(1, -1),
+            stencil_codes.T, coarse_ids.reshape(1, -1), cotangent,
+            encode_weight, process_weight, coarse_weight, decode_weight,
+        )
+    )
+
+
+def any_size(*args):
+    groups = lax.axis_size("mesh") * lax.axis_size("tile")
+    row_count, c_in = args[0].shape
+    nodes = MA * MB * groups
+    aligned = row_count % 128 == 0 and args[3].shape[1] == EXTRA
+    fits = nodes <= min(256, c_in + args[9].shape[1]) and aligned and lax.axis_size("feat") == 2
+    return (replicated_body if fits else body)(*args)
+
+
 def solution(mesh):
     placed = (
         P(("parts", "mesh", "tile"), None),
@@ -216,7 +504,7 @@
         P(("parts", "mesh", "tile"), None),
     )
     return jax.shard_map(
-        body,
+        any_size,
         mesh=mesh,
         in_specs=placed,
         out_specs=(

time: 240 us -> 27.7 us (0.12)
  waiting for transfers between devices: 116 us -> 0 us
  blocking collectives: 47.2 us -> 0 us
  starting transfers between devices: 37.2 us -> 0 us
  Pallas kernels: 0 us -> 21.1 us
  between operations: 14 us -> 0.66 us
  matrix products: 13.2 us -> 0 us
  local copies, waits for them, and re-layouts: 8.52 us -> 5.77 us
  other arithmetic: 2.47 us -> 0 us
    psum x2 -> x0, waiting for transfers between devices: 93.1 us -> none  [the longest x1 73.2 us: body(): lax.psum((encode_grad, process_grad, decode_grad), ('mesh', 'tile'))]
    psum x1 -> x0, blocking collectives: 26.2 us -> none  [body(): coarse_total = lax.psum(coarse_part, ('mesh', 'tile'))]
    all_to_all x5 -> x0, starting transfers between devices: 22.4 us -> none  [the longest x3 10.3 us: route_block(): lax.all_to_all(block.reshape(flat_shape), ('mesh', 'tile'), split_axis=0,...]
    pallas_call x0 -> x1, Pallas kernels: none -> 21.1 us  [replicated_body(): pl.pallas_call(functools.partial(step_kernel, mesh_count, tile_count), ou...]
    all_gather x4 -> x0, blocking collectives: 21 us -> none  [the longest x1 9.03 us: body(): lax.all_gather(coarse_total.astype(jnp.bfloat16), 'feat', axis=1, tiled=T...]
    ppermute x12 -> x0, starting transfers between devices: 14.7 us -> none  [the longest x6 11.6 us: padded(): after = lax.ppermute(initial, axis, down)]
    all_to_all x5 -> x0, waiting for transfers between devices: 13.5 us -> none  [the longest x3 8.8 us: route_block(): lax.all_to_all(block.reshape(flat_shape), ('mesh', 'tile'), split_axis=0,...]
    dot_general x22 -> x0, matrix products: 13.2 us -> none  [the longest x1 1.21 us: body(): jnp.dot(agg_full.astype(jnp.float32).T, grad_pre_mesh, precision=highest)]
  transfers between devices with their start and end apart: 20 -> 0, of which waited for: 11 -> 0; matrix products, arithmetic and copies ran while one was open for 6% -> 0% of each run, Pallas kernels for 0% -> 0%
where the time goes in v2:
time: 27.7 us; the launch traced here: 27.5 us
  Pallas kernels  21.1 us (76%)
  local copies, waits for them, and re-layouts  5.77 us (21%)
  between operations  0.66 us (2%)
    pallas_call x1, Pallas kernels, replicated_body(): pl.pallas_call(functools.partial(step_kernel, mesh_count, tile_count), ou...  21.1 us
    unnamed x11, local copies, waits for them, and re-layouts  5.77 us

profile of v2, /device:TPU:1, one launch (start us, length us, event | category | flops | bytes accessed | tf_op | source)
XLA Modules:
  0.0 27.5 jit_solution(16663314487467453660)
XLA Ops:
  0.6 21.1 %step.1 = (f32[128,128]{1,0:T(8,128)}, f32[128,256]{1,0:T(8,128)}, f32[512,256]{1,0:T(8,128)}, f32[512,256]{1,0:T(8,128)}, f32[256,128]{1,0:T(8,128)}) custom-call(bf16[128,128]{1,0:T(8,128)(2,1)} %fields.1, s32[1,128]{1,0:T(1,128)} %bitcast.5, s32[1,128]{1,0:T(1,128)} %bitcast.6, s32[8,32]{1,0:T(8,128)} %bitcast.4, s32[1,32]{1,0:T(1,128)} %bitcast.7, ...), custom_call_target="tpu_custom_call" | custom-call | tf_op jit(solution)/shard_map/step/pallas_call | solution.py:447
  21.7 0.0 copy-start.2
  21.7 1.5 %copy.20 = f32[128,128]{1,0:T(8,128)} copy(f32[128,128]{1,0:T(8,128)} %get-tuple-element.10) | data formatting | bytes 131072
  23.3 0.0 copy-done.2
  23.3 0.7 %copy.21 = f32[128,256]{1,0:T(8,128)} copy(f32[128,256]{1,0:T(8,128)S(1)} %copy-done.2) | data formatting | bytes 262144
  23.9 0.0 copy-start
  23.9 1.9 %copy.22 = f32[512,256]{1,0:T(8,128)} copy(f32[512,256]{1,0:T(8,128)} %get-tuple-element.12) | data formatting | bytes 1048576
  25.8 0.0 copy-done
  25.8 0.0 copy-start.1
  25.8 0.8 %copy.23 = f32[512,256]{1,0:T(8,128)} copy(f32[512,256]{1,0:T(8,128)S(1)} %copy-done) | data formatting | bytes 1048576
  26.6 0.2 copy-done.1
  26.9 0.7 %copy.24 = f32[256,128]{1,0:T(8,128)} copy(f32[256,128]{1,0:T(8,128)S(1)} %copy-done.1) | data formatting | bytes 262144
Async XLA Ops:
  21.7 1.5 %copy-start.2 = (f32[128,256]{1,0:T(8,128)S(1)}, f32[128,256]{1,0:T(8,128)}, u32[]{:S(2)}) copy-start(f32[128,256]{1,0:T(8,128)} %get-tuple-element.11) | copy-start | bytes 393220
  23.9 1.9 %copy-start = (f32[512,256]{1,0:T(8,128)S(1)}, f32[512,256]{1,0:T(8,128)}, u32[]{:S(2)}) copy-start(f32[512,256]{1,0:T(8,128)} %get-tuple-element.13) | copy-start | bytes 1572868
  25.8 1.0 %copy-start.1 = (f32[256,128]{1,0:T(8,128)S(1)}, f32[256,128]{1,0:T(8,128)}, u32[]{:S(2)}) copy-start(f32[256,128]{1,0:T(8,128)} %get-tuple-element.14) | copy-start | bytes 393220

commit v3 on v2

--- a/solution.py
+++ b/solution.py
@@ -209,7 +209,7 @@
 MESH = pl.DeviceIdType.MESH
 ROW_DIMS = (((0,), (0,)), ((), ()))
 COL_DIMS = (((1,), (1,)), ((), ()))
-EXTRA = 8
+IDS = 8
 
 
 def quotient(values, divisor):
@@ -237,9 +237,10 @@
     mesh_count, tile_count,
     fields, owner_group, owner_node, codes, coarse_ids, cotangent,
     enc_n, proc_n, coarse_n, dec_n,
-    prediction, encode_grad, process_grad, coarse_grad, decode_grad,
-    gath, enc, proc, coarse, dec, cells, cot, attach, pre_s, hid_s, base_s, one_s, two_s, gpm_s, gpc_s,
-    send_sem, recv_sem, pass_send, pass_recv, weight_send, weight_recv, local_sem,
+    prediction, encode_grad, decode_grad, agg_out, gpm_out, coarse_in_out, gpc_out,
+    gath, gath_cot, enc, proc, coarse, dec, cells, cot, attach, pre_s, hid_s, slope_s, one_s, two_s, gpm_s, gpc_s,
+    send_sem, recv_sem, pass_send, pass_recv, cot_send, cot_recv, cot_pass_send, cot_pass_recv,
+    weight_send, weight_recv, local_sem,
 ):
     f32, b16 = jnp.float32, jnp.bfloat16
     groups = mesh_count * tile_count
@@ -250,7 +251,7 @@
     nodes = nodes_local * groups
     coarse_count = CPD * groups
     row_count, c_in = fields.shape
-    width = c_in + cotangent.shape[1]
+    width = 2 * row_count
     part_rows = row_count // 2
     half = enc_n.shape[1]
     mine = pl.ds(pl.multiple_of(feat * half, half), half)
@@ -275,9 +276,10 @@
         copy.start()
         locals_.append(copy)
 
-    both = jnp.concatenate([fields[...], cotangent[...].astype(b16)], axis=1)
-    gath[me, 0, :part_rows, :] = both[:part_rows]
-    gath[me, 1, :part_rows, :] = both[part_rows:]
+    own_cot = cotangent[...].astype(b16)
+    for h in range(2):
+        gath[me, h, :part_rows, :] = fields[h * part_rows : (h + 1) * part_rows, :]
+        gath_cot[me, h] = own_cot[h * part_rows : (h + 1) * part_rows]
     code = codes[...]
     code_row = sum(jnp.where(code >= 5 * i, 1, 0) for i in range(1, 5))
     local = lax.broadcasted_iota(jnp.int32, (1, nodes_local), 1)
@@ -298,25 +300,44 @@
         == lax.broadcasted_iota(jnp.int32, (nodes_local, width), 0) + nodes_local * me,
         1.0, 0.0,
     ).astype(b16)
-    order = lax.broadcasted_iota(jnp.int32, (EXTRA, nodes_local), 0)
+    order = lax.broadcasted_iota(jnp.int32, (IDS, nodes_local), 0)
     owned = jnp.where(order == 1, coarse_ids[...], 0).astype(f32).astype(b16)
     owned = dot(owned, spot)
     target = (owner_group[...] * nodes_local + owner_node[...]).astype(f32)
-    order = lax.broadcasted_iota(jnp.int32, (EXTRA, row_count), 0)
+    order = lax.broadcasted_iota(jnp.int32, (IDS, row_count), 0)
     named = jnp.where(order == 0, target, owned[:, :row_count])
-    gath[me, 0, part_rows:, :] = jnp.concatenate([named, owned[:, row_count:]], axis=1).astype(b16)
-    gath[me, 1, part_rows:, :] = dot(near.astype(f32).astype(b16), spot).astype(b16)
+    linked = dot(near.astype(f32).astype(b16), spot)
+    gath[me, 0, part_rows:, :] = jnp.concatenate([named, owned[:, row_count:]], axis=0).astype(b16)
+    gath[me, 1, part_rows:, :] = jnp.concatenate(
+        [linked[:, :row_count], linked[:, row_count:]], axis=0
+    ).astype(b16)
 
     pl.semaphore_wait(barrier, groups)
-    sends = []
-    for d in range(1, groups):
+
+    def spread(buffer, send, recv):
+        copies = []
+        for d in range(1, groups):
+            copy = pltpu.make_async_remote_copy(
+                src_ref=buffer.at[me, feat], dst_ref=buffer.at[me, feat],
+                send_sem=send.at[d], recv_sem=recv.at[d],
+                device_id=place((me + d) % groups), device_id_type=MESH,
+            )
+            copy.start()
+            copies.append(copy)
+        return copies
+
+    def hand_on(buffer, d, send, recv):
+        came = (me - d + groups) % groups
         copy = pltpu.make_async_remote_copy(
-            src_ref=gath.at[me, feat], dst_ref=gath.at[me, feat],
-            send_sem=send_sem.at[d], recv_sem=recv_sem.at[d],
-            device_id=place((me + d) % groups), device_id_type=MESH,
+            src_ref=buffer.at[came, feat], dst_ref=buffer.at[came, feat],
+            send_sem=send.at[d], recv_sem=recv.at[d],
+            device_id=sibling, device_id_type=MESH,
         )
         copy.start()
-        sends.append(copy)
+        return copy
+
+    sends = spread(gath, send_sem, recv_sem)
+    cot_sends = spread(gath_cot, cot_send, cot_recv)
     weights = []
     for i, (src, dst) in enumerate(pairs):
         copy = pltpu.make_async_remote_copy(
@@ -327,34 +348,29 @@
         copy.start()
         weights.append(copy)
 
+    def span(g):
+        return pl.ds(pl.multiple_of(g * row_count, row_count), row_count)
+
     def take(g):
-        rows = pl.ds(pl.multiple_of(g * row_count, row_count), row_count)
-        block = jnp.concatenate([gath[g, h, :part_rows, :] for h in range(2)], axis=0)
-        x, c = block[:, :c_in], block[:, c_in:]
+        rows = span(g)
+        x = jnp.concatenate([gath[g, h, :part_rows, :] for h in range(2)], axis=0)
         cells[rows, :] = x
-        cot[rows, :] = c
-        ids = gath[g, 0, part_rows:, :][:1, :row_count].astype(f32).astype(jnp.int32)
+        ids = gath[g, 0, part_rows:, :][:1, :].astype(f32).astype(jnp.int32)
         attach[:, rows] = onehot(ids, nodes).astype(b16)
         pre = dot(x, enc[...])
-        pre_s[rows, :] = pre
+        pre_s[...] = pre
         hid_s[rows, :] = (pre * jax.nn.sigmoid(pre)).astype(b16)
-        base_s[rows, :] = col_dot(c, dec[mine, :])
-
-    for i in range(2):
-        locals_[i].wait()
-        weights[i].wait_recv()
+        own = pre_s[:, mine]
+        sig = jax.nn.sigmoid(own)
+        slope_s[rows, :] = sig * (1.0 + own * (1.0 - sig))
+
+    locals_[0].wait()
+    weights[0].wait_recv()
     passes = []
     take(me)
     for d in range(1, groups):
         sends[d - 1].wait_recv()
-        came = (me - d + groups) % groups
-        copy = pltpu.make_async_remote_copy(
-            src_ref=gath.at[came, feat], dst_ref=gath.at[came, feat],
-            send_sem=pass_send.at[d], recv_sem=pass_recv.at[d],
-            device_id=sibling, device_id_type=MESH,
-        )
-        copy.start()
-        passes.append(copy)
+        passes.append(hand_on(gath, d, pass_send, pass_recv))
         if d > 1:
             passes[d - 2].wait_recv()
             take((me - d + 1 + groups) % groups)
@@ -362,20 +378,26 @@
     take((me + 1) % groups)
 
     node_in = dot(attach[...], hid_s[...]).astype(b16)
-    node_cot = dot(attach[...], cot[...]).astype(b16)
     owned = gath[0, 0, part_rows:, :].astype(f32)
     linked = gath[0, 1, part_rows:, :].astype(f32)
     for g in range(1, groups):
         owned = owned + gath[g, 0, part_rows:, :].astype(f32)
         linked = linked + gath[g, 1, part_rows:, :].astype(f32)
-    linked = linked[:, :nodes].astype(jnp.int32)
+    owned = jnp.concatenate([owned[:IDS], owned[IDS:]], axis=1)
+    linked = jnp.concatenate([linked[:IDS], linked[IDS:]], axis=1)[:, :nodes].astype(jnp.int32)
     edges = onehot(linked[0:1], nodes)
-    for k in range(1, linked.shape[0]):
+    for k in range(1, IDS):
         edges = edges + onehot(linked[k : k + 1], nodes)
     edges = edges.astype(b16)
     to_coarse = onehot(owned[1:2, :nodes].astype(jnp.int32), coarse_count).astype(b16)
 
+    cot_passes = []
+    for d in range(1, groups):
+        cot_sends[d - 1].wait_recv()
+        cot_passes.append(hand_on(gath_cot, d, cot_pass_send, cot_pass_recv))
+
     agg = row_dot(edges, node_in).astype(b16)
+    agg_out[...] = agg
     locals_[2].wait()
     weights[2].wait_recv()
     pre_mesh = dot(agg, proc[...])
@@ -392,7 +414,13 @@
     level_two = (level_one + row_dot(to_coarse, coarse_out)).astype(b16)
     two_s[...] = level_two
 
-    own_rows = pl.ds(pl.multiple_of(me * row_count, row_count), row_count)
+    own_rows = span(me)
+    locals_[1].wait()
+    weights[1].wait_recv()
+    for copy in cot_passes:
+        copy.wait_recv()
+    cot[...] = gath_cot[...].reshape(cot.shape)
+    node_cot = dot(attach[...], cot[...]).astype(b16)
     merged = (
         hid_s[own_rows, :].astype(f32) + row_dot(attach[:, own_rows], level_two)
     ).astype(b16)
@@ -407,23 +435,33 @@
     )
     gpc = grad_pre_coarse.astype(b16)
     gpc_s[...] = gpc
-    coarse_grad[...] = row_dot(coarse_in, gpc_s[:, mine])
+    coarse_in_out[...] = coarse_in
+    gpc_out[...] = gpc_s[:, mine]
     grad_coarse_in = col_dot(gpc, coarse[...]).astype(b16)
     grad_one = grad_two + row_dot(to_coarse, grad_coarse_in)
     one_s[...] = grad_one
     gpm = (grad_one * (sig_mesh * (1.0 + pre_mesh * (1.0 - sig_mesh)))).astype(b16)
     gpm_s[...] = gpm
-    process_grad[...] = row_dot(agg, gpm_s[:, mine])
+    gpm_out[...] = gpm_s[:, mine]
     grad_agg = col_dot(gpm, proc[mine, :]).astype(b16)
     grad_zero = (one_s[:, mine] + dot(edges, grad_agg)).astype(b16)
-    grad_hidden = base_s[...] + row_dot(attach[...], grad_zero)
-    pre_own = pre_s[:, mine]
-    sig_own = jax.nn.sigmoid(pre_own)
-    grad_pre = (grad_hidden * (sig_own * (1.0 + pre_own * (1.0 - sig_own)))).astype(b16)
+    grad_hidden = col_dot(cot[...], dec[mine, :]) + row_dot(attach[...], grad_zero)
+    grad_pre = (grad_hidden * slope_s[...]).astype(b16)
     encode_grad[...] = row_dot(cells[...], grad_pre)
 
-    for copy in sends + passes + weights:
+    for copy in sends + passes + cot_sends + cot_passes + weights:
         copy.wait_send()
+
+
+def product_kernel(
+    pred_in, encode_in, decode_in, agg, gpm, coarse_in, gpc,
+    prediction, encode_grad, process_grad, coarse_grad, decode_grad,
+):
+    prediction[...] = pred_in[...]
+    encode_grad[...] = encode_in[...]
+    decode_grad[...] = decode_in[...]
+    process_grad[...] = row_dot(agg[...], gpm[...])
+    coarse_grad[...] = row_dot(coarse_in[...], gpc[...])
 
 
 def replicated_body(
@@ -443,41 +481,55 @@
     any_spec = pl.BlockSpec(memory_space=pl.ANY)
     vmem = pl.BlockSpec(memory_space=pltpu.VMEM)
     shape = lambda *dims: jax.ShapeDtypeStruct(dims, f32)
+    short = lambda *dims: jax.ShapeDtypeStruct(dims, b16)
+    part_rows = row_count // 2
+    parts = pl.pallas_call(
+        functools.partial(step_kernel, mesh_count, tile_count),
+        out_shape=[
+            shape(row_count, c_out), shape(c_in, half), shape(half, c_out),
+            short(nodes, full), short(nodes, half), short(coarse_count, full),
+            short(coarse_count, half),
+        ],
+        in_specs=[vmem] * 6 + [any_spec] * 4,
+        out_specs=[vmem] * 7,
+        scratch_shapes=[
+            pltpu.VMEM((groups, 2, part_rows + 2 * IDS, c_in), b16),
+            pltpu.VMEM((groups, 2, part_rows, c_out), b16),
+            pltpu.VMEM((c_in, full), b16),
+            pltpu.VMEM((full, full), b16),
+            pltpu.VMEM((full, full), b16),
+            pltpu.VMEM((full, c_out), b16),
+            pltpu.VMEM((total_rows, c_in), b16),
+            pltpu.VMEM((total_rows, c_out), b16),
+            pltpu.VMEM((nodes, total_rows), b16),
+            pltpu.VMEM((row_count, full), f32),
+            pltpu.VMEM((total_rows, full), b16),
+            pltpu.VMEM((total_rows, half), f32),
+            pltpu.VMEM((nodes, full), f32),
+            pltpu.VMEM((nodes, full), b16),
+            pltpu.VMEM((nodes, full), b16),
+            pltpu.VMEM((coarse_count, full), b16),
+        ]
+        + [pltpu.SemaphoreType.DMA((groups,))] * 8
+        + [pltpu.SemaphoreType.DMA((4,))] * 3,
+        compiler_params=pltpu.CompilerParams(collective_id=0, has_side_effects=True),
+        name="step",
+    )(
+        fields, owner_group.reshape(1, -1), owner_node.reshape(1, -1),
+        stencil_codes.T, coarse_ids.reshape(1, -1), cotangent,
+        encode_weight, process_weight, coarse_weight, decode_weight,
+    )
     return tuple(
         pl.pallas_call(
-            functools.partial(step_kernel, mesh_count, tile_count),
+            product_kernel,
             out_shape=[
                 shape(row_count, c_out), shape(c_in, half), shape(full, half),
                 shape(full, half), shape(half, c_out),
             ],
-            in_specs=[vmem] * 6 + [any_spec] * 4,
+            in_specs=[vmem] * 7,
             out_specs=[vmem] * 5,
-            scratch_shapes=[
-                pltpu.VMEM((groups, 2, row_count // 2 + EXTRA, c_in + c_out), b16),
-                pltpu.VMEM((c_in, full), b16),
-                pltpu.VMEM((full, full), b16),
-                pltpu.VMEM((full, full), b16),
-                pltpu.VMEM((full, c_out), b16),
-                pltpu.VMEM((total_rows, c_in), b16),
-                pltpu.VMEM((total_rows, c_out), b16),
-                pltpu.VMEM((nodes, total_rows), b16),
-                pltpu.VMEM((total_rows, full), f32),
-                pltpu.VMEM((total_rows, full), b16),
-                pltpu.VMEM((total_rows, half), f32),
-                pltpu.VMEM((nodes, full), f32),
-                pltpu.VMEM((nodes, full), b16),
-                pltpu.VMEM((nodes, full), b16),
-                pltpu.VMEM((coarse_count, full), b16),
-            ]
-            + [pltpu.SemaphoreType.DMA((groups,))] * 4
-            + [pltpu.SemaphoreType.DMA((4,))] * 3,
-            compiler_params=pltpu.CompilerParams(collective_id=0, has_side_effects=True),
-            name="step",
-        )(
-            fields, owner_group.reshape(1, -1), owner_node.reshape(1, -1),
-            stencil_codes.T, coarse_ids.reshape(1, -1), cotangent,
-            encode_weight, process_weight, coarse_weight, decode_weight,
-        )
+            name="products",
+        )(*parts)
     )
 
 
@@ -485,8 +537,8 @@
     groups = lax.axis_size("mesh") * lax.axis_size("tile")
     row_count, c_in = args[0].shape
     nodes = MA * MB * groups
-    aligned = row_count % 128 == 0 and args[3].shape[1] == EXTRA
-    fits = nodes <= min(256, c_in + args[9].shape[1]) and aligned and lax.axis_size("feat") == 2
+    aligned = row_count % 128 == 0 and c_in == row_count and args[3].shape[1] == IDS
+    fits = nodes <= min(256, 2 * row_count) and aligned and lax.axis_size("feat") == 2
     return (replicated_body if fits else body)(*args)
 
 

time: 27.7 us -> 23.7 us (0.86)
  local copies, waits for them, and re-layouts: 5.77 us -> 0 us
  Pallas kernels: 21.1 us -> 22.8 us
    unnamed x11 -> x0, local copies, waits for them, and re-layouts: 5.77 us -> none
    pallas_call x0 -> x1, Pallas kernels: none -> 2.5 us  [replicated_body(): pl.pallas_call(product_kernel, out_shape=[shape(row_count, c_out), shape(...]
    pallas_call x1, Pallas kernels: 21.1 us -> 20.3 us  [replicated_body(): pl.pallas_call(functools.partial(step_kernel, mesh_count, tile_count), ou...]
where the time goes in v3:
time: 23.7 us; the launch traced here: 23.4 us
  Pallas kernels  22.8 us (96%)
  between operations  0.64 us (3%)
    pallas_call x1, Pallas kernels, replicated_body(): pl.pallas_call(functools.partial(step_kernel, mesh_count, tile_count), ou...  20.3 us
    pallas_call x1, Pallas kernels, replicated_body(): pl.pallas_call(product_kernel, out_shape=[shape(row_count, c_out), shape(...  2.5 us

profile of v3, /device:TPU:1, one launch (start us, length us, event | category | flops | bytes accessed | tf_op | source)
XLA Modules:
  0.0 23.4 jit_solution(10990242227658366400)
XLA Ops:
  0.6 20.3 %step.1 = (f32[128,128]{1,0:T(8,128)}, f32[128,256]{1,0:T(8,128)}, f32[256,128]{1,0:T(8,128)}, bf16[256,512]{1,0:T(8,128)(2,1)}, bf16[256,256]{1,0:T(8,128)(2,1)...) custom-call(bf16[128,128]{1,0:T(8,128)(2,1)} %fields.1, s32[1,128]{1,0:T(1,128)} %bitcast.5, s32[1,128]{1,0:T(1,128)} %bitcast.6, ...), custom_call_target="tpu_custom_call" | custom-call | tf_op jit(solution)/shard_map/step/pallas_call | solution.py:486
  20.9 2.5 %products.1 = (f32[128,128]{1,0:T(8,128)}, f32[128,256]{1,0:T(8,128)}, f32[512,256]{1,0:T(8,128)}, f32[512,256]{1,0:T(8,128)}, f32[256,128]{1,0:T(8,128)}) custom-call(f32[128,128]{1,0:T(8,128)} %get-tuple-element.12.pred_in, f32[128,256]{1,0:T(8,128)} %get-tuple-element.13.encode_in, f32[256,128]{1,0:T(8,128)} %get-tuple-element.14.decode_in, ...), custom_call_target="tpu_custom_call" | custom-call | tf_op jit(solution)/shard_map/products/pallas_call | solution.py:523

commit v4 on v3

--- a/solution.py
+++ b/solution.py
@@ -235,12 +235,13 @@
 
 def step_kernel(
     mesh_count, tile_count,
-    fields, owner_group, owner_node, codes, coarse_ids, cotangent,
+    fields_in, owner_group_in, owner_node_in, codes_in, coarse_ids_in, cotangent_in,
     enc_n, proc_n, coarse_n, dec_n,
     prediction, encode_grad, decode_grad, agg_out, gpm_out, coarse_in_out, gpc_out,
     gath, gath_cot, enc, proc, coarse, dec, cells, cot, attach, pre_s, hid_s, slope_s, one_s, two_s, gpm_s, gpc_s,
     send_sem, recv_sem, pass_send, pass_recv, cot_send, cot_recv, cot_pass_send, cot_pass_recv,
     weight_send, weight_recv, local_sem,
+    fields, owner_group, owner_node, codes, coarse_ids, cotangent, input_sem,
 ):
     f32, b16 = jnp.float32, jnp.bfloat16
     groups = mesh_count * tile_count
@@ -270,12 +271,23 @@
         (enc_n, enc.at[:, mine]), (dec_n, dec.at[mine, :]),
         (proc_n, proc.at[:, mine]), (coarse_n, coarse.at[:, mine]),
     )
+    inputs = (
+        (codes_in, codes), (coarse_ids_in, coarse_ids), (owner_group_in, owner_group),
+        (owner_node_in, owner_node), (fields_in, fields), (cotangent_in, cotangent),
+    )
+    loads = []
+    for i, (src, dst) in enumerate(inputs):
+        copy = pltpu.make_async_copy(src, dst, input_sem.at[i])
+        copy.start()
+        loads.append(copy)
     locals_ = []
     for i, (src, dst) in enumerate(pairs):
         copy = pltpu.make_async_copy(src, dst, local_sem.at[i])
         copy.start()
         locals_.append(copy)
 
+    for copy in loads:
+        copy.wait()
     own_cot = cotangent[...].astype(b16)
     for h in range(2):
         gath[me, h, :part_rows, :] = fields[h * part_rows : (h + 1) * part_rows, :]
@@ -377,6 +389,10 @@
     passes[groups - 2].wait_recv()
     take((me + 1) % groups)
 
+    cot_passes = []
+    for d in range(1, groups):
+        cot_sends[d - 1].wait_recv()
+        cot_passes.append(hand_on(gath_cot, d, cot_pass_send, cot_pass_recv))
     node_in = dot(attach[...], hid_s[...]).astype(b16)
     owned = gath[0, 0, part_rows:, :].astype(f32)
     linked = gath[0, 1, part_rows:, :].astype(f32)
@@ -390,11 +406,6 @@
         edges = edges + onehot(linked[k : k + 1], nodes)
     edges = edges.astype(b16)
     to_coarse = onehot(owned[1:2, :nodes].astype(jnp.int32), coarse_count).astype(b16)
-
-    cot_passes = []
-    for d in range(1, groups):
-        cot_sends[d - 1].wait_recv()
-        cot_passes.append(hand_on(gath_cot, d, cot_pass_send, cot_pass_recv))
 
     agg = row_dot(edges, node_in).astype(b16)
     agg_out[...] = agg
@@ -481,16 +492,16 @@
     any_spec = pl.BlockSpec(memory_space=pl.ANY)
     vmem = pl.BlockSpec(memory_space=pltpu.VMEM)
     shape = lambda *dims: jax.ShapeDtypeStruct(dims, f32)
-    short = lambda *dims: jax.ShapeDtypeStruct(dims, b16)
     part_rows = row_count // 2
     parts = pl.pallas_call(
         functools.partial(step_kernel, mesh_count, tile_count),
         out_shape=[
-            shape(row_count, c_out), shape(c_in, half), shape(half, c_out),
-            short(nodes, full), short(nodes, half), short(coarse_count, full),
-            short(coarse_count, half),
+            pltpu.VMEM((row_count, c_out), f32), pltpu.VMEM((c_in, half), f32),
+            pltpu.VMEM((half, c_out), f32), pltpu.VMEM((nodes, full), b16),
+            pltpu.VMEM((nodes, half), b16), pltpu.VMEM((coarse_count, full), b16),
+            pltpu.VMEM((coarse_count, half), b16),
         ],
-        in_specs=[vmem] * 6 + [any_spec] * 4,
+        in_specs=[any_spec] * 10,
         out_specs=[vmem] * 7,
         scratch_shapes=[
             pltpu.VMEM((groups, 2, part_rows + 2 * IDS, c_in), b16),
@@ -511,7 +522,16 @@
             pltpu.VMEM((coarse_count, full), b16),
         ]
         + [pltpu.SemaphoreType.DMA((groups,))] * 8
-        + [pltpu.SemaphoreType.DMA((4,))] * 3,
+        + [pltpu.SemaphoreType.DMA((4,))] * 3
+        + [
+            pltpu.VMEM((row_count, c_in), b16),
+            pltpu.VMEM((1, row_count), jnp.int32),
+            pltpu.VMEM((1, row_count), jnp.int32),
+            pltpu.VMEM((IDS, MA * MB), jnp.int32),
+            pltpu.VMEM((1, MA * MB), jnp.int32),
+            pltpu.VMEM((row_count, c_out), f32),
+            pltpu.SemaphoreType.DMA((6,)),
+        ],
         compiler_params=pltpu.CompilerParams(collective_id=0, has_side_effects=True),
         name="step",
     )(
@@ -528,6 +548,7 @@
             ],
             in_specs=[vmem] * 7,
             out_specs=[vmem] * 5,
+            compiler_params=pltpu.CompilerParams(vmem_limit_bytes=32 * 2**20),
             name="products",
         )(*parts)
     )

time: 23.7 us -> 21.2 us (0.89)
  Pallas kernels: 22.8 us -> 20.4 us
    pallas_call x1, Pallas kernels: 20.3 us -> 19.1 us  [replicated_body(): pl.pallas_call(functools.partial(step_kernel, mesh_count, tile_count), ou...]
    pallas_call x1, Pallas kernels: 2.5 us -> 1.33 us  [replicated_body(): pl.pallas_call(product_kernel, out_shape=[shape(row_count, c_out), shape(...]
where the time goes in v4:
time: 21.2 us; the launch traced here: 21.1 us
  Pallas kernels  20.4 us (96%)
  between operations  0.64 us (3%)
    pallas_call x1, Pallas kernels, replicated_body(): pl.pallas_call(functools.partial(step_kernel, mesh_count, tile_count), ou...  19.1 us
    pallas_call x1, Pallas kernels, replicated_body(): pl.pallas_call(product_kernel, out_shape=[shape(row_count, c_out), shape(...  1.33 us

profile of v4, /device:TPU:1, one launch (start us, length us, event | category | flops | bytes accessed | tf_op | source)
XLA Modules:
  0.0 21.1 jit_solution(12688464504832883921)
XLA Ops:
  0.6 19.1 %step.1 = (f32[128,128]{1,0:T(8,128)S(1)}, f32[128,256]{1,0:T(8,128)S(1)}, f32[256,128]{1,0:T(8,128)S(1)}, bf16[256,512]{1,0:T(8,128)(2,1)S(1)}, bf16[256,256]{1...) custom-call(bf16[128,128]{1,0:T(8,128)(2,1)} %fields_in.1, s32[1,128]{1,0:T(1,128)} %bitcast.5, ...), custom_call_target="tpu_custom_call" | custom-call | tf_op jit(solution)/shard_map/step/pallas_call | solution.py:496
  19.7 1.3 %products.1 = (f32[128,128]{1,0:T(8,128)}, f32[128,256]{1,0:T(8,128)}, f32[512,256]{1,0:T(8,128)}, f32[512,256]{1,0:T(8,128)}, f32[256,128]{1,0:T(8,128)}) custom-call(f32[128,128]{1,0:T(8,128)S(1)} %get-tuple-element.12.pred_in, f32[128,256]{1,0:T(8,128)S(1)} %get-tuple-element.13.encode_in, f32[256,128]{1,0:T(8,128)S(1)} %get-tuple-element.14.decode_in, ...), custom_call_target="tpu_custom_call" | custom-call | tf_op jit(solution)/shard_map/products/pallas_call | solution.py:543
